TPU v7x, 128 devices: a whole 4x4x4 slice. The times are simulated.
128 devices in a mesh: row: 32 (over x, y, core), col: 4 (over z).
Axes of the slice: x: 4, y: 4, z: 4, core: 2. Of those that a mesh axis runs over, the one named last changes fastest.
Arguments:
- kernel: float32 [16384, 16384], P('row', 'col'), may hold values from -7 to 7, as said below
- nugget: float32 [16384], P('row'), may hold values from 0.25 to 1
Outputs:
- factored: float32 [16384, 16384], P('row', 'col')
Inputs may be any that keep to these rules, and one draw needn't show every extreme that they name: In matrix order the kernel is symmetric and positive semidefinite.
All inputs are finite; a program needn't handle non-finite values.
Results may differ from a plain program's by a relative error of at most 0.0018.
Values may be sent and summed in bfloat16 or wider, within the bound.
A program may use at most 192 MiB of HBM per device.

v0:
```python
import jax
import jax.numpy as jnp
from jax import lax
from jax.sharding import PartitionSpec as P

B = 256
STEPS = 7


def broadcast(value, axis, source):
    kept = jnp.where(lax.axis_index(axis) == source, value, 0).astype(value.dtype)
    return lax.psum(kept, axis)


def apply_step(columns, row_side, col_part, later_rows, at_rows, later_cols):
    product = jnp.dot(row_side, col_part.T, preferred_element_type=jnp.float32)
    reduced = jnp.where(later_rows[:, None] & later_cols[None, :], columns - product, columns)
    return jnp.where(at_rows[:, None] & later_cols[None, :], jnp.float32(0.0), reduced)


def update_range(matrix, row_side, col_side, later_rows, at_rows, later_cols):
    return apply_step(matrix, row_side, col_side, later_rows, at_rows, later_cols)


def body(kernel, nugget):
    rows_here, cols_here = kernel.shape
    tile_width = B
    grid_rows = lax.axis_size("row")
    grid_cols = lax.axis_size("col")
    row_pos = lax.axis_index("row")
    col_pos = lax.axis_index("col")
    row_tiles = rows_here // tile_width
    row_offsets = jnp.arange(rows_here, dtype=jnp.int32)
    col_offsets = jnp.arange(cols_here, dtype=jnp.int32)
    row_tile_of = row_offsets // tile_width * grid_rows + row_pos
    col_tile_of = col_offsets // tile_width * grid_cols + col_pos
    same_entry = (row_tile_of[:, None] == col_tile_of[None, :]) & (
        (row_offsets % tile_width)[:, None] == (col_offsets % tile_width)[None, :]
    )
    matrix = kernel + jnp.where(same_entry, nugget[:, None], jnp.float32(0.0))
    for panel_step in range(STEPS):
        root_row = panel_step % grid_rows
        root_col = panel_step % grid_cols
        row_slot = panel_step // grid_rows
        col_slot = panel_step // grid_cols
        panel_strip = matrix[:, col_slot * tile_width : (col_slot + 1) * tile_width]
        diag_local = panel_strip[row_slot * tile_width : (row_slot + 1) * tile_width]
        diag_tile = broadcast(diag_local, "row", root_row)
        factor = jnp.linalg.cholesky(diag_tile)
        solved = lax.linalg.triangular_solve(
            factor, panel_strip, left_side=False, lower=True, transpose_a=True
        )
        row_side = broadcast(solved.astype(jnp.bfloat16), "col", root_col)
        share_rows = rows_here // grid_cols
        own_share = lax.dynamic_slice_in_dim(row_side, col_pos * share_rows, share_rows, 0)
        gathered = lax.all_gather(own_share[None], "row", axis=0, tiled=True)
        grouped = gathered.reshape(grid_rows // grid_cols, grid_cols, 1, share_rows, tile_width)
        regrouped = lax.all_to_all(grouped, "col", split_axis=1, concat_axis=2, tiled=True)
        owners = regrouped.reshape(grid_rows // grid_cols, row_tiles, tile_width, tile_width)
        col_side = jnp.transpose(owners, (1, 0, 2, 3)).reshape(cols_here, tile_width)
        later_rows = row_tile_of > panel_step
        at_rows = row_tile_of == panel_step
        later_cols = col_tile_of > panel_step
        is_root = col_pos == root_col
        stacked_factor = jnp.tile(factor, (row_tiles, 1))
        panel_lo = col_slot * tile_width
        panel_hi = panel_lo + tile_width
        updated = update_range(matrix, row_side, col_side, later_rows, at_rows, later_cols)
        columns = updated[:, panel_lo:panel_hi]
        panel_value = jnp.where(
            later_rows[:, None], solved, jnp.where(at_rows[:, None], stacked_factor, columns)
        )
        matrix = updated.at[:, panel_lo:panel_hi].set(jnp.where(is_root, panel_value, columns))
    return matrix


def solution(mesh):
    return jax.shard_map(
        body,
        mesh=mesh,
        in_specs=(P("row", "col"), P("row")),
        out_specs=P("row", "col"),
        check_vma=False,
    )
```

profile of v0, /device:TPU:1, one launch (start us, length us, event | category | flops | bytes accessed | tf_op | source)
XLA Modules:
  0.0 2154.9 jit_solution(4204105284378569621)
XLA Ops:
  6.6 9.0 copy.93
  15.5 6.7 select_add_fusion
  26.4 104.3 %all-reduce.16.cloned.1.call-done = f32[256,256]{0,1:T(8,128)} async-done(((f32[256,256]{0,1:T(8,128)}), f32[256,256]{0,1:T(8,128)}) %all-reduce.16.cloned.1.call-update) | async-done | bytes 262160 | tf_op jit(solution)/shard_map/psum | solution.py:12
  132.8 11.7 cholesky.340
  144.6 9.8 custom-call.23
  154.9 11.7 cholesky.357
  173.9 19.7 custom-call.24
  197.6 39.7 %all-reduce.18.cloned.1.call-done = bf16[512,256]{0,1:T(8,128)(2,1)} async-done(((bf16[512,256]{0,1:T(8,128)(2,1)}), bf16[512,256]{0,1:T(8,128)(2,1)}) %all-reduce.18.cloned.1.call-update) | async-done | bytes 262160 | tf_op jit(solution)/shard_map/psum | solution.py:12
  238.8 48.2 %all-gather.15.cloned.1.call-done = bf16[4096,256]{0,1:T(8,128)(2,1)} async-done(((bf16[128,256]{0,1:T(8,128)(2,1)}), bf16[4096,256]{0,1:T(8,128)(2,1)}) %all-gather.15.cloned.1.call-update) | async-done | bytes 2097168 | tf_op jit(solution)/shard_map/all_gather | solution.py:56
  298.2 24.8 %all-to-all-done = bf16[8,4,1,128,256]{4,3,0,2,1:T(8,128)(2,1)S(1)} async-done(((bf16[8,4,1,128,256]{4,3,0,2,1:T(8,128)(2,1)}), bf16[8,4,1,128,256]{4,3,0,2,1:T(8,128)(2,1)S(1)}, u32[]{:S(2)}, u32[]{:S(2)}) %all-to-all-start) | async-done | bytes 2097184 | tf_op jit(solution)/shard_map/all_to_all | solution.py:58
  324.1 6.7 fusion
  334.3 99.4 %all-reduce.20.cloned.1.call-done = f32[256,256]{0,1:T(8,128)} async-done(((f32[256,256]{0,1:T(8,128)}), f32[256,256]{0,1:T(8,128)}) %all-reduce.20.cloned.1.call-update) | async-done | bytes 262160 | tf_op jit(solution)/shard_map/psum | solution.py:12
  435.8 11.7 cholesky.374
  447.6 9.8 custom-call.25
  457.9 11.7 cholesky.391
  476.5 19.7 custom-call.26
  498.3 39.7 %all-reduce.22.cloned.1.call-done = bf16[512,256]{0,1:T(8,128)(2,1)} async-done(((bf16[512,256]{0,1:T(8,128)(2,1)}), bf16[512,256]{0,1:T(8,128)(2,1)}) %all-reduce.22.cloned.1.call-update) | async-done | bytes 262160 | tf_op jit(solution)/shard_map/psum | solution.py:12
  539.5 48.1 %all-gather.17.cloned.1.call-done = bf16[4096,256]{0,1:T(8,128)(2,1)} async-done(((bf16[128,256]{0,1:T(8,128)(2,1)}), bf16[4096,256]{0,1:T(8,128)(2,1)}) %all-gather.17.cloned.1.call-update) | async-done | bytes 2097168 | tf_op jit(solution)/shard_map/all_gather | solution.py:56
  598.1 25.5 %all-to-all-done.1 = bf16[8,4,1,128,256]{4,3,0,2,1:T(8,128)(2,1)S(1)} async-done(((bf16[8,4,1,128,256]{4,3,0,2,1:T(8,128)(2,1)}), bf16[8,4,1,128,256]{4,3,0,2,1:T(8,128)(2,1)S(1)}, u32[]{:S(2)}, u32[]{:S(2)}) %all-to-all-start.1) | async-done | bytes 2097184 | tf_op jit(solution)/shard_map/all_to_all | solution.py:58
  624.6 6.7 fusion.1
  635.0 99.1 %all-reduce.24.cloned.1.call-done = f32[256,256]{0,1:T(8,128)} async-done(((f32[256,256]{0,1:T(8,128)}), f32[256,256]{0,1:T(8,128)}) %all-reduce.24.cloned.1.call-update) | async-done | bytes 262160 | tf_op jit(solution)/shard_map/psum | solution.py:12
  736.3 11.7 cholesky.408
  748.0 9.8 custom-call.27
  758.3 11.7 cholesky.425
  777.1 19.7 custom-call.28
  798.8 39.7 %all-reduce.26.cloned.1.call-done = bf16[512,256]{0,1:T(8,128)(2,1)} async-done(((bf16[512,256]{0,1:T(8,128)(2,1)}), bf16[512,256]{0,1:T(8,128)(2,1)}) %all-reduce.26.cloned.1.call-update) | async-done | bytes 262160 | tf_op jit(solution)/shard_map/psum | solution.py:12
  840.0 48.2 %all-gather.19.cloned.1.call-done = bf16[4096,256]{0,1:T(8,128)(2,1)} async-done(((bf16[128,256]{0,1:T(8,128)(2,1)}), bf16[4096,256]{0,1:T(8,128)(2,1)}) %all-gather.19.cloned.1.call-update) | async-done | bytes 2097168 | tf_op jit(solution)/shard_map/all_gather | solution.py:56
  898.8 25.5 %all-to-all-done.2 = bf16[8,4,1,128,256]{4,3,0,2,1:T(8,128)(2,1)S(1)} async-done(((bf16[8,4,1,128,256]{4,3,0,2,1:T(8,128)(2,1)}), bf16[8,4,1,128,256]{4,3,0,2,1:T(8,128)(2,1)S(1)}, u32[]{:S(2)}, u32[]{:S(2)}) %all-to-all-start.2) | async-done | bytes 2097184 | tf_op jit(solution)/shard_map/all_to_all | solution.py:58
  925.3 6.7 fusion.2
  936.0 98.9 %all-reduce.28.cloned.1.call-done = f32[256,256]{0,1:T(8,128)} async-done(((f32[256,256]{0,1:T(8,128)}), f32[256,256]{0,1:T(8,128)}) %all-reduce.28.cloned.1.call-update) | async-done | bytes 262160 | tf_op jit(solution)/shard_map/psum | solution.py:12
  1037.0 11.7 cholesky.442
  1048.7 9.8 custom-call.29
  1059.0 11.7 cholesky.459
  1077.7 19.7 custom-call.30
  1099.5 39.7 %all-reduce.30.cloned.1.call-done = bf16[512,256]{0,1:T(8,128)(2,1)} async-done(((bf16[512,256]{0,1:T(8,128)(2,1)}), bf16[512,256]{0,1:T(8,128)(2,1)}) %all-reduce.30.cloned.1.call-update) | async-done | bytes 262160 | tf_op jit(solution)/shard_map/psum | solution.py:12
  1140.7 48.1 %all-gather.21.cloned.1.call-done = bf16[4096,256]{0,1:T(8,128)(2,1)} async-done(((bf16[128,256]{0,1:T(8,128)(2,1)}), bf16[4096,256]{0,1:T(8,128)(2,1)}) %all-gather.21.cloned.1.call-update) | async-done | bytes 2097168 | tf_op jit(solution)/shard_map/all_gather | solution.py:56
  1199.3 25.5 %all-to-all-done.3 = bf16[8,4,1,128,256]{4,3,0,2,1:T(8,128)(2,1)S(1)} async-done(((bf16[8,4,1,128,256]{4,3,0,2,1:T(8,128)(2,1)}), bf16[8,4,1,128,256]{4,3,0,2,1:T(8,128)(2,1)S(1)}, u32[]{:S(2)}, u32[]{:S(2)}) %all-to-all-start.3) | async-done | bytes 2097184 | tf_op jit(solution)/shard_map/all_to_all | solution.py:58
  1236.5 99.1 %all-reduce.32.cloned.1.call-done = f32[256,256]{0,1:T(8,128)} async-done(((f32[256,256]{0,1:T(8,128)}), f32[256,256]{0,1:T(8,128)}) %all-reduce.32.cloned.1.call-update) | async-done | bytes 262160 | tf_op jit(solution)/shard_map/psum | solution.py:12
  1337.8 11.7 cholesky.476
  1349.5 9.8 custom-call.31
  1359.8 11.7 cholesky.493
  1378.6 19.7 custom-call.32
  1402.2 39.7 %all-reduce.34.cloned.1.call-done = bf16[512,256]{0,1:T(8,128)(2,1)} async-done(((bf16[512,256]{0,1:T(8,128)(2,1)}), bf16[512,256]{0,1:T(8,128)(2,1)}) %all-reduce.34.cloned.1.call-update) | async-done | bytes 262160 | tf_op jit(solution)/shard_map/psum | solution.py:12
  1443.4 48.0 %all-gather.23.cloned.1.call-done = bf16[4096,256]{0,1:T(8,128)(2,1)} async-done(((bf16[128,256]{0,1:T(8,128)(2,1)}), bf16[4096,256]{0,1:T(8,128)(2,1)}) %all-gather.23.cloned.1.call-update) | async-done | bytes 2097168 | tf_op jit(solution)/shard_map/all_gather | solution.py:56
  1502.7 24.9 %all-to-all-done.4 = bf16[8,4,1,128,256]{4,3,0,2,1:T(8,128)(2,1)S(1)} async-done(((bf16[8,4,1,128,256]{4,3,0,2,1:T(8,128)(2,1)}), bf16[8,4,1,128,256]{4,3,0,2,1:T(8,128)(2,1)S(1)}, u32[]{:S(2)}, u32[]{:S(2)}) %all-to-all-start.4) | async-done | bytes 2097184 | tf_op jit(solution)/shard_map/all_to_all | solution.py:58
  1528.6 6.7 fusion.4
  1539.2 99.0 %all-reduce.36.cloned.1.call-done = f32[256,256]{0,1:T(8,128)} async-done(((f32[256,256]{0,1:T(8,128)}), f32[256,256]{0,1:T(8,128)}) %all-reduce.36.cloned.1.call-update) | async-done | bytes 262160 | tf_op jit(solution)/shard_map/psum | solution.py:12
  1640.2 11.7 cholesky.510
  1652.0 9.8 custom-call.33
  1662.3 11.7 cholesky.527
  1681.0 19.7 custom-call.34
  1702.7 39.7 %all-reduce.38.cloned.1.call-done = bf16[512,256]{0,1:T(8,128)(2,1)} async-done(((bf16[512,256]{0,1:T(8,128)(2,1)}), bf16[512,256]{0,1:T(8,128)(2,1)}) %all-reduce.38.cloned.1.call-update) | async-done | bytes 262160 | tf_op jit(solution)/shard_map/psum | solution.py:12
  1743.9 48.1 %all-gather.25.cloned.1.call-done = bf16[4096,256]{0,1:T(8,128)(2,1)} async-done(((bf16[128,256]{0,1:T(8,128)(2,1)}), bf16[4096,256]{0,1:T(8,128)(2,1)}) %all-gather.25.cloned.1.call-update) | async-done | bytes 2097168 | tf_op jit(solution)/shard_map/all_gather | solution.py:56
  1802.5 25.5 %all-to-all-done.5 = bf16[8,4,1,128,256]{4,3,0,2,1:T(8,128)(2,1)S(1)} async-done(((bf16[8,4,1,128,256]{4,3,0,2,1:T(8,128)(2,1)}), bf16[8,4,1,128,256]{4,3,0,2,1:T(8,128)(2,1)S(1)}, u32[]{:S(2)}, u32[]{:S(2)}) %all-to-all-start.5) | async-done | bytes 2097184 | tf_op jit(solution)/shard_map/all_to_all | solution.py:58
  1829.1 6.7 fusion.5
  1839.4 99.2 %all-reduce.40.cloned.1.call-done = f32[256,256]{0,1:T(8,128)} async-done(((f32[256,256]{0,1:T(8,128)}), f32[256,256]{0,1:T(8,128)}) %all-reduce.40.cloned.1.call-update) | async-done | bytes 262160 | tf_op jit(solution)/shard_map/psum | solution.py:12
  1940.7 11.7 cholesky.544
  1952.4 9.8 custom-call.35
  1962.7 11.7 cholesky.561
  1981.5 19.7 custom-call.36
  2003.2 39.7 %all-reduce.42.cloned.1.call-done = bf16[512,256]{0,1:T(8,128)(2,1)} async-done(((bf16[512,256]{0,1:T(8,128)(2,1)}), bf16[512,256]{0,1:T(8,128)(2,1)}) %all-reduce.42.cloned.1.call-update) | async-done | bytes 262160 | tf_op jit(solution)/shard_map/psum | solution.py:12
  2044.4 48.2 %all-gather.27.cloned.1.call-done = bf16[4096,256]{0,1:T(8,128)(2,1)} async-done(((bf16[128,256]{0,1:T(8,128)(2,1)}), bf16[4096,256]{0,1:T(8,128)(2,1)}) %all-gather.27.cloned.1.call-update) | async-done | bytes 2097168 | tf_op jit(solution)/shard_map/all_gather | solution.py:56
  2103.2 25.5 %all-to-all-done.6 = bf16[8,4,1,128,256]{4,3,0,2,1:T(8,128)(2,1)S(1)} async-done(((bf16[8,4,1,128,256]{4,3,0,2,1:T(8,128)(2,1)}), bf16[8,4,1,128,256]{4,3,0,2,1:T(8,128)(2,1)S(1)}, u32[]{:S(2)}, u32[]{:S(2)}) %all-to-all-start.6) | async-done | bytes 2097184 | tf_op jit(solution)/shard_map/all_to_all | solution.py:58
  2138.9 8.9 copy.143
  (322 shorter events, 239.5 us)
Async XLA Ops:
  6.5 124.2 %all-reduce.16.cloned.1.call-start = ((), (), s32[]{:S(2)}) async-start(), calls=%async_computation.7 | async-start | bytes 524288 | tf_op jit(solution)/shard_map/psum | solution.py:12
  6.6 9.0 copy-start.9
  22.2 3.4 copy-start.1
  26.4 210.9 %all-reduce.18.cloned.1.call-start = ((), (), s32[]{:S(2)}) async-start(), calls=%async_computation.8 | async-start | bytes 524288 | tf_op jit(solution)/shard_map/psum | solution.py:12
  197.5 89.5 %all-gather.15.cloned.1.call-start = ((), (), s32[]{:S(2)}) async-start(), calls=%async_computation.21 | async-start | bytes 2162688 | tf_op jit(solution)/shard_map/all_gather | solution.py:56
  293.0 30.0 %all-to-all-start = ((bf16[8,4,1,128,256]{4,3,0,2,1:T(8,128)(2,1)}), bf16[8,4,1,128,256]{4,3,0,2,1:T(8,128)(2,1)S(1)}, u32[]{:S(2)}, u32[]{:S(2)}) async-start(bf16[8,4,1,128,256]{4,3,0,2,1:T(8,128)(2,1)} %copy.96), calls=%async_computation | async-start | bytes 4194304 | tf_op jit(solution)/shard_map/all_to_all | solution.py:58
  297.1 136.6 %all-reduce.20.cloned.1.call-start = ((), (), s32[]{:S(2)}) async-start(), calls=%async_computation.9 | async-start | bytes 524288 | tf_op jit(solution)/shard_map/psum | solution.py:12
  323.1 1.0 copy-start.2
  334.2 203.8 %all-reduce.22.cloned.1.call-start = ((), (), s32[]{:S(2)}) async-start(), calls=%async_computation.10 | async-start | bytes 524288 | tf_op jit(solution)/shard_map/psum | solution.py:12
  498.2 89.3 %all-gather.17.cloned.1.call-start = ((), (), s32[]{:S(2)}) async-start(), calls=%async_computation.22 | async-start | bytes 2162688 | tf_op jit(solution)/shard_map/all_gather | solution.py:56
  593.5 30.0 %all-to-all-start.1 = ((bf16[8,4,1,128,256]{4,3,0,2,1:T(8,128)(2,1)}), bf16[8,4,1,128,256]{4,3,0,2,1:T(8,128)(2,1)S(1)}, u32[]{:S(2)}, u32[]{:S(2)}) async-start(bf16[8,4,1,128,256]{4,3,0,2,1:T(8,128)(2,1)} %copy.103), calls=%async_computation.1 | async-start | bytes 4194304 | tf_op jit(solution)/shard_map/all_to_all | solution.py:58
  597.7 136.5 %all-reduce.24.cloned.1.call-start = ((), (), s32[]{:S(2)}) async-start(), calls=%async_computation.11 | async-start | bytes 524288 | tf_op jit(solution)/shard_map/psum | solution.py:12
  623.7 1.0 copy-start.6
  634.8 203.8 %all-reduce.26.cloned.1.call-start = ((), (), s32[]{:S(2)}) async-start(), calls=%async_computation.12 | async-start | bytes 524288 | tf_op jit(solution)/shard_map/psum | solution.py:12
  798.8 89.4 %all-gather.19.cloned.1.call-start = ((), (), s32[]{:S(2)}) async-start(), calls=%async_computation.23 | async-start | bytes 2162688 | tf_op jit(solution)/shard_map/all_gather | solution.py:56
  894.2 30.0 %all-to-all-start.2 = ((bf16[8,4,1,128,256]{4,3,0,2,1:T(8,128)(2,1)}), bf16[8,4,1,128,256]{4,3,0,2,1:T(8,128)(2,1)S(1)}, u32[]{:S(2)}, u32[]{:S(2)}) async-start(bf16[8,4,1,128,256]{4,3,0,2,1:T(8,128)(2,1)} %copy.110), calls=%async_computation.2 | async-start | bytes 4194304 | tf_op jit(solution)/shard_map/all_to_all | solution.py:58
  898.4 136.5 %all-reduce.28.cloned.1.call-start = ((), (), s32[]{:S(2)}) async-start(), calls=%async_computation.13 | async-start | bytes 524288 | tf_op jit(solution)/shard_map/psum | solution.py:12
  924.4 1.0 copy-start.7
  935.5 203.7 %all-reduce.30.cloned.1.call-start = ((), (), s32[]{:S(2)}) async-start(), calls=%async_computation.14 | async-start | bytes 524288 | tf_op jit(solution)/shard_map/psum | solution.py:12
  1099.4 89.3 %all-gather.21.cloned.1.call-start = ((), (), s32[]{:S(2)}) async-start(), calls=%async_computation.24 | async-start | bytes 2162688 | tf_op jit(solution)/shard_map/all_gather | solution.py:56
  1194.7 30.0 %all-to-all-start.3 = ((bf16[8,4,1,128,256]{4,3,0,2,1:T(8,128)(2,1)}), bf16[8,4,1,128,256]{4,3,0,2,1:T(8,128)(2,1)S(1)}, u32[]{:S(2)}, u32[]{:S(2)}) async-start(bf16[8,4,1,128,256]{4,3,0,2,1:T(8,128)(2,1)} %copy.117), calls=%async_computation.3 | async-start | bytes 4194304 | tf_op jit(solution)/shard_map/all_to_all | solution.py:58
  1198.9 136.8 %all-reduce.32.cloned.1.call-start = ((), (), s32[]{:S(2)}) async-start(), calls=%async_computation.15 | async-start | bytes 524288 | tf_op jit(solution)/shard_map/psum | solution.py:12
  1224.9 1.0 copy-start.3
  1232.1 3.4 copy-start
  1236.3 205.7 %all-reduce.34.cloned.1.call-start = ((), (), s32[]{:S(2)}) async-start(), calls=%async_computation.16 | async-start | bytes 524288 | tf_op jit(solution)/shard_map/psum | solution.py:12
  1402.2 89.3 %all-gather.23.cloned.1.call-start = ((), (), s32[]{:S(2)}) async-start(), calls=%async_computation.25 | async-start | bytes 2162688 | tf_op jit(solution)/shard_map/all_gather | solution.py:56
  1497.5 30.0 %all-to-all-start.4 = ((bf16[8,4,1,128,256]{4,3,0,2,1:T(8,128)(2,1)}), bf16[8,4,1,128,256]{4,3,0,2,1:T(8,128)(2,1)S(1)}, u32[]{:S(2)}, u32[]{:S(2)}) async-start(bf16[8,4,1,128,256]{4,3,0,2,1:T(8,128)(2,1)} %copy.124), calls=%async_computation.4 | async-start | bytes 4194304 | tf_op jit(solution)/shard_map/all_to_all | solution.py:58
  1501.6 136.5 %all-reduce.36.cloned.1.call-start = ((), (), s32[]{:S(2)}) async-start(), calls=%async_computation.17 | async-start | bytes 524288 | tf_op jit(solution)/shard_map/psum | solution.py:12
  1527.6 1.0 copy-start.4
  1538.7 203.8 %all-reduce.38.cloned.1.call-start = ((), (), s32[]{:S(2)}) async-start(), calls=%async_computation.18 | async-start | bytes 524288 | tf_op jit(solution)/shard_map/psum | solution.py:12
  1702.7 89.3 %all-gather.25.cloned.1.call-start = ((), (), s32[]{:S(2)}) async-start(), calls=%async_computation.26 | async-start | bytes 2162688 | tf_op jit(solution)/shard_map/all_gather | solution.py:56
  1798.0 30.0 %all-to-all-start.5 = ((bf16[8,4,1,128,256]{4,3,0,2,1:T(8,128)(2,1)}), bf16[8,4,1,128,256]{4,3,0,2,1:T(8,128)(2,1)S(1)}, u32[]{:S(2)}, u32[]{:S(2)}) async-start(bf16[8,4,1,128,256]{4,3,0,2,1:T(8,128)(2,1)} %copy.131), calls=%async_computation.5 | async-start | bytes 4194304 | tf_op jit(solution)/shard_map/all_to_all | solution.py:58
  1802.1 136.5 %all-reduce.40.cloned.1.call-start = ((), (), s32[]{:S(2)}) async-start(), calls=%async_computation.19 | async-start | bytes 524288 | tf_op jit(solution)/shard_map/psum | solution.py:12
  1828.1 1.0 copy-start.5
  1839.2 203.8 %all-reduce.42.cloned.1.call-start = ((), (), s32[]{:S(2)}) async-start(), calls=%async_computation.20 | async-start | bytes 524288 | tf_op jit(solution)/shard_map/psum | solution.py:12
  2003.2 89.4 %all-gather.27.cloned.1.call-start = ((), (), s32[]{:S(2)}) async-start(), calls=%async_computation.27 | async-start | bytes 2162688 | tf_op jit(solution)/shard_map/all_gather | solution.py:56
  2098.6 30.0 %all-to-all-start.6 = ((bf16[8,4,1,128,256]{4,3,0,2,1:T(8,128)(2,1)}), bf16[8,4,1,128,256]{4,3,0,2,1:T(8,128)(2,1)S(1)}, u32[]{:S(2)}, u32[]{:S(2)}) async-start(bf16[8,4,1,128,256]{4,3,0,2,1:T(8,128)(2,1)} %copy.138), calls=%async_computation.6 | async-start | bytes 4194304 | tf_op jit(solution)/shard_map/all_to_all | solution.py:58
  2128.8 1.0 copy-start.8
Sparse Core Ops, SparseCore 0:
  26.5 104.1 all-reduce.15
  197.6 39.6 all-reduce.17
  239.5 47.4 all-gather.14
  334.3 99.3 all-reduce.19
  498.4 39.5 all-reduce.21
  540.0 47.4 all-gather.16
  634.9 99.2 all-reduce.23
  798.9 39.5 all-reduce.25
  840.7 47.4 all-gather.18
  935.6 99.2 all-reduce.27
  1099.5 39.6 all-reduce.29
  1141.2 47.4 all-gather.20
  1236.4 99.2 all-reduce.31
  1402.3 39.6 all-reduce.33
  1444.0 47.4 all-gather.22
  1538.8 99.3 all-reduce.35
  1702.8 39.5 all-reduce.37
  1744.5 47.4 all-gather.24
  1839.3 99.2 all-reduce.39
  2003.3 39.5 all-reduce.41
  2045.1 47.4 all-gather.26
where the time goes:
time: 2170 us; the launch traced here: 2150 us
  waiting for transfers between devices  1490 us (69%)
  other arithmetic  422 us (19%)
  local copies, waits for them, and re-layouts  123 us (6%)
  matrix products  61.4 us (3%)
  starting transfers between devices  31.1 us (1%)
  between operations  24 us (1%)
    psum x14, waiting for transfers between devices, broadcast(): return lax.psum(kept, axis)  977 us
    all_gather x7, waiting for transfers between devices, body(): gathered = lax.all_gather(own_share[None], 'row', axis=0, tiled=True)  337 us
    another operation x49, other arithmetic, body(): factor = jnp.linalg.cholesky(diag_tile)  243 us
    all_to_all x7, waiting for transfers between devices, body(): lax.all_to_all(grouped, 'col', split_axis=1, concat_axis=2, tiled=True)  177 us
    another operation x15, other arithmetic, body(): lax.linalg.triangular_solve(factor, panel_strip, left_side=False, lower=T...  138 us
    dot_general x7, matrix products, apply_step(): product = jnp.dot(row_side, col_part.T, preferred_element_type=jnp.float32)  45.7 us
  transfers between devices with their start and end apart: 28, of which 28 were waited for; matrix products, arithmetic and copies ran while one was open for 0% of the time, Pallas kernels for 0%

commit v1 on v0

v1 whole, which is shorter than its diff:
```python
import jax
import jax.numpy as jnp
from jax import lax
from jax.experimental import pallas as pl
from jax.experimental.pallas import tpu as pltpu
from jax.sharding import PartitionSpec as P

B = 256
H = 128
STEPS = 7
F32 = jnp.float32
BF16 = jnp.bfloat16
MESH = pl.DeviceIdType.MESH
NT = (((1,), (1,)), ((), ()))
NN = (((1,), (0,)), ((), ()))


def dot_full(a, b, dims):
    return lax.dot_general(a, b, dims, precision=lax.Precision.HIGHEST, preferred_element_type=F32)


def dot_bf(a, b, dims):
    return lax.dot_general(a, b, dims, preferred_element_type=F32)


def lane_splat(x, at):
    return jnp.broadcast_to(x[:, at : at + 1], x.shape)


def row_splat(x, at):
    return jnp.broadcast_to(x[at : at + 1, :], x.shape)


def inverse_factor(groups):
    lane = lax.broadcasted_iota(jnp.int32, (8, H), 1)
    sub = lax.broadcasted_iota(jnp.int32, (8, H), 0)
    groups = list(groups)
    result = []
    for b in range(16):
        start = 8 * b
        block = (lane >= start) & (lane < start + 8)
        here = groups[b]
        cols = [lane_splat(here, start + s) for s in range(8)]
        swept = jnp.where(block, jnp.where(lane - start == sub, 1.0, 0.0), here)
        scaled = jnp.zeros((8, H), F32)
        for r in range(8):
            pivot = row_splat(cols[r], r)
            inv = 1.0 / pivot
            row = row_splat(swept, r)
            at_r = sub == r
            scaled = jnp.where(at_r, row * lax.rsqrt(pivot), scaled)
            row = row * inv
            swept = jnp.where(at_r, row, swept - cols[r] * row)
            for j in range(r + 1, 8):
                entry = row_splat(cols[j], r) * inv
                cols[j] = jnp.where(at_r, entry, cols[j] - cols[r] * entry)
        result.append(jnp.where(lane <= sub + start, scaled, 0.0))
        rows = [row_splat(swept, s) for s in range(8)]
        for g in range(b + 1, 16):
            terms = [lane_splat(groups[g], start + s) * rows[s] for s in range(8)]
            while len(terms) > 1:
                terms = [terms[i] + terms[i + 1] for i in range(0, len(terms), 2)]
            groups[g] = jnp.where(block, 0.0, groups[g]) - terms[0]
    return result


def chain_kernel(lead_ref, lead_bf_ref, inv_ref, tiles, diag, inv_half, low, mixed):
    for t in range(28):
        x, y, c = t // 8, t // 2 % 4, t % 2
        tiles[t] = lead_ref[0, x, y] if c == 0 else lead_ref[1, y, x]

    def step(k, carry):
        at = k * (k + 1) // 2 + k

        def half(h, carry):
            @pl.when(h == 0)
            def _():
                diag[...] = tiles[at, 0:H, 0:H]

            done = inverse_factor([diag[8 * g : 8 * g + 8, :] for g in range(16)])
            for g in range(16):
                inv_half[8 * g : 8 * g + 8, :] = done[g]

            @pl.when(h == 0)
            def _():
                first = inv_half[...]
                l21 = dot_full(tiles[at, H:B, 0:H], first, NT)
                diag[...] = tiles[at, H:B, H:B] - dot_full(l21, l21, NT)
                mixed[...] = dot_full(l21, first, NN)
                inv_ref[k, 0:H, 0:H] = first
                inv_ref[k, 0:H, H:B] = jnp.zeros((H, H), F32)

            @pl.when(h == 1)
            def _():
                second = inv_half[...]
                inv_ref[k, H:B, 0:H] = -dot_full(second, mixed[...], NN)
                inv_ref[k, H:B, H:B] = second

            return carry

        lax.fori_loop(0, 2, half, 0)

        def solve(i, carry):
            t = i * (i + 1) // 2 + k
            lead_bf_ref[t] = dot_full(tiles[t], inv_ref[k], NT).astype(BF16)
            return carry

        lax.fori_loop(k + 1, STEPS, solve, 0)

        def update_row(i, carry):
            left = lead_bf_ref[i * (i + 1) // 2 + k]

            def update(j, carry):
                t = i * (i + 1) // 2 + j
                tiles[t] = tiles[t] - dot_bf(left, lead_bf_ref[j * (j + 1) // 2 + k], NT)
                return carry

            return lax.fori_loop(k + 1, i + 1, update, carry)

        return lax.fori_loop(k + 1, STEPS, update_row, carry)

    lax.fori_loop(0, STEPS, step, 0)


def chain(lead):
    vmem = pl.BlockSpec(memory_space=pltpu.VMEM)
    return pl.pallas_call(
        chain_kernel,
        out_shape=(
            jax.ShapeDtypeStruct((28, B, B), BF16),
            jax.ShapeDtypeStruct((STEPS, B, B), F32),
        ),
        in_specs=[vmem],
        out_specs=(vmem, vmem),
        scratch_shapes=[
            pltpu.VMEM((28, B, B), F32),
            pltpu.VMEM((H, H), F32),
            pltpu.VMEM((H, H), F32),
            pltpu.VMEM((H, H), F32),
            pltpu.VMEM((H, H), F32),
        ],
        compiler_params=pltpu.CompilerParams(vmem_limit_bytes=56 * 2**20),
    )(lead)


def place(row):
    core, y, x = row % 2, row // 2 % 4, row // 8
    return core, x * (1 - core) + y * core, y * (1 - core) + x * core


def row_of(core, major, minor):
    x = major * (1 - core) + minor * core
    y = minor * (1 - core) + major * core
    return (x * 4 + y) * 2 + core


def walk_plane(out_ref, send, recv):
    row, col = lax.axis_index("row"), lax.axis_index("col")
    core, major, minor = place(row)

    def copy(ref, to_core, to_major, to_minor, slot):
        return pltpu.make_async_remote_copy(
            src_ref=ref,
            dst_ref=ref,
            send_sem=send.at[slot],
            recv_sem=recv.at[slot],
            device_id=(row_of(to_core, to_major, to_minor), col),
            device_id_type=MESH,
        )

    def ring(block, half_low, half_high, me, device, base):
        after, before = (me + 1) % 4, (me + 3) % 4
        own_up = copy(block(me), *device(after), base)
        own_down = copy(block(me), *device(before), base + 1)
        own_up.start()
        own_down.start()
        own_up.wait_recv()
        far_up = copy(half_low(before), *device(after), base + 2)
        far_up.start()
        own_down.wait_recv()
        far_down = copy(half_high(after), *device(before), base + 3)
        far_down.start()
        return [own_up, own_down, far_up, far_down]

    half = out_ref.shape[3] // 2
    first = ring(
        lambda at: out_ref.at[core, major, at],
        lambda at: out_ref.at[core, major, at, pl.ds(0, half)],
        lambda at: out_ref.at[core, major, at, pl.ds(half, half)],
        minor,
        lambda at: (core, major, at),
        0,
    )
    for entry in first[2:]:
        entry.wait_recv()
    for entry in first:
        entry.wait_send()
    other = 1 - core
    sibling = (other, major * 0 + place(row + 1 - 2 * core)[1], place(row + 1 - 2 * core)[2])
    across = [copy(out_ref.at[core, major], *sibling, 8)]
    across[0].start()
    second = ring(
        lambda at: out_ref.at[core, at],
        lambda at: out_ref.at[core, at, pl.ds(0, 2)],
        lambda at: out_ref.at[core, at, pl.ds(2, 2)],
        major,
        lambda at: (core, at, minor),
        4,
    )
    for step, at in ((9, (major + 3) % 4), (10, (major + 1) % 4)):
        entry = copy(out_ref.at[core, at], *sibling, step)
        entry.start()
        across.append(entry)
    for entry in second[2:]:
        entry.wait_recv()
    entry = copy(out_ref.at[core, (major + 2) % 4], *sibling, 11)
    entry.start()
    across.append(entry)
    for entry in across:
        entry.wait_recv()
    for entry in second + across:
        entry.wait_send()


def lead_kernel(strip_ref, out_ref, fill_send, fill_recv, own_sem, send, recv):
    row, col = lax.axis_index("row"), lax.axis_index("col")
    core, major, minor = place(row)
    is_own = (row >= 28) | ((col == 0) & (row < 2))

    def fill(u, plane, to):
        to_core, to_major, to_minor = place(to)
        return pltpu.make_async_remote_copy(
            src_ref=strip_ref.at[u, pl.ds(0, B)],
            dst_ref=out_ref.at[to_core, to_major, to_minor],
            send_sem=fill_send.at[u, plane],
            recv_sem=fill_recv,
            device_id=(to, plane),
            device_id_type=MESH,
        )

    cases = []
    for u in range(2):
        to = row * (row + 1) // 2 + col + 4 * u
        for plane in range(4):
            cases.append((u, plane, to, (row < STEPS) & (col + 4 * u <= row) & ((to != row) | (col != plane))))
    for u, plane, to, active in cases:
        @pl.when(active)
        def _(u=u, plane=plane, to=to):
            fill(u, plane, to).start()

    @pl.when(is_own)
    def _():
        own = pltpu.make_async_copy(strip_ref.at[0, pl.ds(0, B)], out_ref.at[core, major, minor], own_sem)
        own.start()
        own.wait()

    @pl.when(jnp.logical_not(is_own))
    def _():
        fill(0, 0, row).wait_recv()

    walk_plane(out_ref, send, recv)
    for u, plane, to, active in cases:
        @pl.when(active)
        def _(u=u, plane=plane, to=to):
            fill(u, plane, to).wait_send()


def side_kernel(rows_ref, out_ref, fill_send, fill_recv, own_sem, send, recv):
    row, col = lax.axis_index("row"), lax.axis_index("col")
    core, major, minor = place(row)
    share = rows_ref.shape[0] // 4
    is_source = row % 4 == col

    def fill(e):
        to = row // 4 * 4 + e
        to_core, to_major, to_minor = place(to)
        return pltpu.make_async_remote_copy(
            src_ref=rows_ref.at[pl.ds(e * share, share)],
            dst_ref=out_ref.at[to_core, to_major, to_minor],
            send_sem=fill_send.at[e],
            recv_sem=fill_recv,
            device_id=(to, col),
            device_id_type=MESH,
        )

    for e in range(4):
        @pl.when(is_source & (col != e))
        def _(e=e):
            fill(e).start()

    @pl.when(is_source)
    def _():
        own = pltpu.make_async_copy(
            rows_ref.at[pl.ds(col * share, share)], out_ref.at[core, major, minor], own_sem
        )
        own.start()
        own.wait()

    @pl.when(jnp.logical_not(is_source))
    def _():
        fill(0).wait_recv()

    walk_plane(out_ref, send, recv)
    for e in range(4):
        @pl.when(is_source & (col != e))
        def _(e=e):
            fill(e).wait_send()


def spread(kernel, operand, block, dtype, fills):
    any_space = pl.BlockSpec(memory_space=pl.ANY)
    return pl.pallas_call(
        kernel,
        out_shape=jax.ShapeDtypeStruct((2, 4, 4) + block, dtype),
        in_specs=[any_space],
        out_specs=any_space,
        scratch_shapes=[
            pltpu.SemaphoreType.DMA(fills),
            pltpu.SemaphoreType.DMA,
            pltpu.SemaphoreType.DMA,
            pltpu.SemaphoreType.DMA((12,)),
            pltpu.SemaphoreType.DMA((12,)),
        ],
        compiler_params=pltpu.CompilerParams(has_side_effects=True),
    )(operand)


def rows_kernel(strips_ref, lead_ref, inv_ref, panel_ref, rounded_ref, acc):
    tile, col = lax.axis_index("row"), lax.axis_index("col")
    at_row = lax.broadcasted_iota(jnp.int32, (2 * B, B), 0)
    at_col = lax.broadcasted_iota(jnp.int32, (2 * B, B), 1)

    def step(k, carry):
        acc[...] = strips_ref[k % 4, k // 4]

        def update(j, carry):
            left = rounded_ref[:, pl.ds(pl.multiple_of(j * B, B), B)]
            acc[...] -= dot_bf(left, lead_ref[k * (k + 1) // 2 + j], NT)
            return carry

        lax.fori_loop(0, k, update, 0)
        solved = dot_full(acc[...], inv_ref[k], NT)
        later = (at_row >= B) | (k < tile)
        rounded_ref[:, pl.ds(pl.multiple_of(k * B, B), B)] = jnp.where(later, solved, 0.0).astype(BF16)

        @pl.when(k % 4 == col)
        def _():
            kept = later | ((k == tile) & (at_col <= at_row))
            panel_ref[k // 4] = jnp.where(kept, solved, 0.0)

        return carry

    lax.fori_loop(0, STEPS, step, 0)


def solve_rows(strips, lead, inv):
    vmem = pl.BlockSpec(memory_space=pltpu.VMEM)
    return pl.pallas_call(
        rows_kernel,
        out_shape=(
            jax.ShapeDtypeStruct((2, 2 * B, B), F32),
            jax.ShapeDtypeStruct((2 * B, STEPS * B), BF16),
        ),
        in_specs=[vmem] * 3,
        out_specs=(vmem, vmem),
        scratch_shapes=[pltpu.VMEM((2 * B, B), F32)],
        compiler_params=pltpu.CompilerParams(vmem_limit_bytes=48 * 2**20),
    )(strips, lead, inv)


def trailing_kernel(matrix_ref, nugget_ref, panel_ref, rounded_ref, even_ref, odd_ref, out_ref):
    slot = pl.program_id(0)
    tile, col = lax.axis_index("row"), lax.axis_index("col")
    col_tile = slot * 4 + col

    @pl.when(col_tile < STEPS)
    def _():
        out_ref[...] = panel_ref[0]

    @pl.when(col_tile >= STEPS)
    def _():
        side = jnp.concatenate([even_ref[0, 0, 0], odd_ref[0, 0, 0]], axis=0)
        for s in range(2):
            rows = pl.ds(s * B, B)
            product = dot_bf(rounded_ref[rows, :], side, NT)
            out_ref[rows, :] = matrix_ref[rows, :] - product

            @pl.when(col_tile == s * 32 + tile)
            def _(s=s, rows=rows):
                at_row = lax.broadcasted_iota(jnp.int32, (B, B), 0)
                at_col = lax.broadcasted_iota(jnp.int32, (B, B), 1)
                out_ref[rows, :] += jnp.where(at_row == at_col, nugget_ref[s : s + 1, :], 0.0)

        @pl.when(tile < STEPS)
        def _():
            out_ref[0:B, :] = jnp.zeros((B, B), F32)


def trailing(matrix, nugget, panel, rounded, side):
    rows, cols = matrix.shape
    depth = rounded.shape[1]

    def even(t):
        return (0, t % 8 // 2, 2 * (t % 2) + t // 8, 0, 0)

    def odd(t):
        return (1, 2 * (t % 2) + t // 8, t % 8 // 2, 0, 0)

    return pl.pallas_call(
        trailing_kernel,
        grid=(cols // B,),
        out_shape=jax.ShapeDtypeStruct(matrix.shape, F32),
        in_specs=[
            pl.BlockSpec((rows, B), lambda t: (0, t)),
            pl.BlockSpec((2, B), lambda t: (0, 0)),
            pl.BlockSpec((1, rows, B), lambda t: (jnp.minimum(t, 1), 0, 0)),
            pl.BlockSpec((rows, depth), lambda t: (0, 0)),
            pl.BlockSpec((1, 1, 1, H, depth), even),
            pl.BlockSpec((1, 1, 1, H, depth), odd),
        ],
        out_specs=pl.BlockSpec((rows, B), lambda t: (0, t)),
        compiler_params=pltpu.CompilerParams(vmem_limit_bytes=48 * 2**20),
    )(matrix, nugget, panel, rounded, side, side)


def body(kernel, nugget):
    rows_here = kernel.shape[0]
    tile, col = lax.axis_index("row"), lax.axis_index("col")
    nugget = nugget.reshape(2, B)
    strip = kernel[:, : 2 * B].reshape(rows_here, 2, B).transpose(1, 0, 2)
    col_tile = jnp.arange(2)[:, None, None] * 4 + col
    same = (
        (col_tile == tile)
        & (jnp.arange(rows_here)[None, :, None] == jnp.arange(B)[None, None, :])
    )
    strip = strip + jnp.where(same, nugget[0][None, None, :], 0.0)
    strips = lax.all_gather(strip, "col")
    lead = spread(lead_kernel, strip, (B, B), F32, (2, 4))
    lead_bf, inv = chain(lead)
    panel, rounded = solve_rows(strips, lead_bf, inv)
    side = spread(side_kernel, rounded, (H, STEPS * B), BF16, (4,))
    return trailing(kernel, nugget, panel, rounded, side)


def solution(mesh):
    return jax.shard_map(
        body,
        mesh=mesh,
        in_specs=(P("row", "col"), P("row")),
        out_specs=P("row", "col"),
        check_vma=False,
    )
```

time: 2170 us -> 339 us (0.16)
  waiting for transfers between devices: 1490 us -> 0.02 us
  other arithmetic: 422 us -> 1.24 us
  Pallas kernels: 0 us -> 318 us
  local copies, waits for them, and re-layouts: 123 us -> 5.41 us
  matrix products: 61.4 us -> 0 us
  starting transfers between devices: 31.1 us -> 0.01 us
    psum x14 -> x0, waiting for transfers between devices: 977 us -> none  [broadcast(): return lax.psum(kept, axis)]
    another operation x66 -> x0, other arithmetic: 382 us -> none  [the longest x49 243 us: body(): factor = jnp.linalg.cholesky(diag_tile)]
    all_gather x7 -> x1, waiting for transfers between devices: 337 us -> 0.01 us  [body(): strips = lax.all_gather(strip, 'col')]
    pallas_call x0 -> x5, Pallas kernels: none -> 318 us  [the longest x2 183 us: spread(): pl.pallas_call(kernel, out_shape=jax.ShapeDtypeStruct((2, 4, 4) + block,...]
    all_to_all x7 -> x0, waiting for transfers between devices: 177 us -> none  [body(): lax.all_to_all(grouped, 'col', split_axis=1, concat_axis=2, tiled=True)]
    dot_general x7 -> x0, matrix products: 45.7 us -> none  [apply_step(): product = jnp.dot(row_side, col_part.T, preferred_element_type=jnp.float32)]
    reshape x14 -> x2, local copies, waits for them, and re-layouts: 41.9 us -> 0.35 us  [the longest x1 0.33 us: body(): strip = kernel[:, :2 * B].reshape(rows_here, 2, B).transpose(1, 0, 2)]
    another operation x71 -> x0, local copies, waits for them, and re-layouts: 29.6 us -> none  [the longest x50 28.2 us: body(): lax.linalg.triangular_solve(factor, panel_strip, left_side=False, lower=T...]
  transfers between devices with their start and end apart: 28 -> 1, of which waited for: 28 -> 0; matrix products, arithmetic and copies ran while one was open for 0% -> 0% of each run, Pallas kernels for 0% -> 56%
where the time goes in v1:
time: 339 us; the launch traced here: 338 us
  Pallas kernels  318 us (94%)
  between operations  13.5 us (4%)
  local copies, waits for them, and re-layouts  5.41 us (2%)
    pallas_call x2, Pallas kernels, spread(): pl.pallas_call(kernel, out_shape=jax.ShapeDtypeStruct((2, 4, 4) + block,...  183 us
    pallas_call x1, Pallas kernels, chain(): pl.pallas_call(chain_kernel, out_shape=(jax.ShapeDtypeStruct((28, B, B),...  96.8 us
    pallas_call x1, Pallas kernels, trailing(): pl.pallas_call(trailing_kernel, grid=(cols // B,), out_shape=jax.ShapeDty...  23.9 us
    pallas_call x1, Pallas kernels, solve_rows(): pl.pallas_call(rows_kernel, out_shape=(jax.ShapeDtypeStruct((2, 2 * B, B)...  13.7 us
  transfers between devices with their start and end apart: 1, of which 0 were waited for; matrix products, arithmetic and copies ran while one was open for 0% of the time, Pallas kernels for 56%

profile of v1, /device:TPU:1, one launch (start us, length us, event | category | flops | bytes accessed | tf_op | source)
XLA Modules:
  0.0 338.0 jit_solution(9386444379836223153)
XLA Ops:
  6.5 0.0 copy-start.3
  6.5 0.0 all-gather.3.cloned.1.call-start
  6.6 0.7 slice.8
  7.3 1.3 slice.7
  8.6 0.3 copy.7
  8.9 0.3 copy.6
  9.3 1.2 bitcast_add_fusion.strip_ref
  10.5 0.0 all-gather.3.cloned.1.call-update
  10.5 0.0 copy-done.3
  10.5 92.2 %shard_map.28.lead_ref = f32[2,4,4,256,256]{4,3,2,1,0:T(8,128)} custom-call(f32[2,512,256]{2,1,0:T(8,128)} %bitcast_add_fusion.strip_ref), custom_call_target="tpu_custom_call" | custom-call | tf_op jit(solution)/shard_map/pallas_call | solution.py:312
  102.7 96.8 %shard_map.29 = (bf16[28,256,256]{2,1,0:T(8,128)(2,1)}, f32[7,256,256]{2,1,0:T(8,128)}) custom-call(f32[2,4,4,256,256]{4,3,2,1,0:T(8,128)} %shard_map.28.lead_ref), custom_call_target="tpu_custom_call" | custom-call | tf_op jit(solution)/shard_map/pallas_call | solution.py:127
  199.5 0.0 all-gather.3.cloned.1.call-done
  199.5 0.0 copy-start.2
  199.5 1.5 copy-done.2
  201.0 13.7 %shard_map.30 = (f32[2,512,256]{2,1,0:T(8,128)S(1)}, bf16[512,1792]{1,0:T(8,128)(2,1)S(1)}) custom-call(f32[4,2,512,256]{3,2,1,0:T(8,128)} %bitcast.4, bf16[28,256,256]{2,1,0:T(8,128)(2,1)} %get-tuple-element.9.lead_ref, f32[7,256,256]{2,1,0:T(8,128)S(1)} %copy-done.2), custom_call_target="tpu_custom_call" | custom-call | tf_op jit(solution)/shard_map/pallas_call | solution.py:358
  214.7 0.0 copy-start
  214.7 1.2 copy-done
  216.0 0.0 copy-start.1
  216.0 91.3 %shard_map.31.even_ref.odd_ref = bf16[2,4,4,128,1792]{4,3,2,1,0:T(8,128)(2,1)} custom-call(bf16[512,1792]{1,0:T(8,128)(2,1)} %copy-done), custom_call_target="tpu_custom_call" | custom-call | tf_op jit(solution)/shard_map/pallas_call | solution.py:312
  307.3 0.0 copy-done.1
  307.3 23.9 %shard_map.32 = f32[512,4096]{1,0:T(8,128)} custom-call(f32[512,4096]{1,0:T(8,128)} %matrix_ref.1, f32[2,256]{1,0:T(2,128)S(1)} %reshape.33.nugget_ref, f32[2,512,256]{2,1,0:T(8,128)S(1)} %get-tuple-element.11.panel_ref, bf16[512,1792]{1,0:T(8,128)(2,1)S(1)} %copy-done.1, bf16[2,4,4,128,1792]{4,3,2,1,0:T(8,128)(2,1)} %shard_map.31.even_ref.odd_ref, ...), custom_call_target="tpu_custom_call" | custom-call | tf_op jit(solution)/shard_map/pallas_call | solution.py:409
  (3 shorter events, 0.1 us)
Async XLA Ops:
  6.5 4.0 %copy-start.3 = (f32[512]{0:T(512)S(1)}, f32[512]{0:T(512)}, u32[]{:S(2)}) copy-start(f32[512]{0:T(512)} %param.3) | copy-start | bytes 6148
  6.5 192.9 %all-gather.3.cloned.1.call-start = ((), (), s32[]{:S(2)}) async-start(), calls=%async_computation | async-start | bytes 5242880 | tf_op jit(solution)/shard_map/all_gather | solution.py:437
  199.5 1.5 copy-start.2
  214.7 1.2 copy-start
  216.0 91.3 %copy-start.1 = (bf16[512,1792]{1,0:T(8,128)(2,1)S(1)}, bf16[512,1792]{1,0:T(8,128)(2,1)}, u32[]{:S(2)}) copy-start(bf16[512,1792]{1,0:T(8,128)(2,1)} %copy-done) | copy-start | bytes 5505028
Sparse Core Ops, SparseCore 0:
  10.6 56.3 all-gather.2

commit v2 on v0

v2 whole, which is shorter than its diff:
```python
import jax
import jax.numpy as jnp
from jax import lax
from jax.experimental import pallas as pl
from jax.experimental.pallas import tpu as pltpu
from jax.sharding import PartitionSpec as P

B = 256
H = 128
STEPS = 7
F32 = jnp.float32
BF16 = jnp.bfloat16
MESH = pl.DeviceIdType.MESH
NT = (((1,), (1,)), ((), ()))
NN = (((1,), (0,)), ((), ()))


def dot_full(a, b, dims):
    return lax.dot_general(a, b, dims, precision=lax.Precision.HIGHEST, preferred_element_type=F32)


def dot_bf(a, b, dims):
    return lax.dot_general(a, b, dims, preferred_element_type=F32)


def lane_splat(x, at):
    return jnp.broadcast_to(x[:, at : at + 1], x.shape)


def row_splat(x, at):
    return jnp.broadcast_to(x[at : at + 1, :], x.shape)


def inverse_factor(groups, hooks):
    lane = lax.broadcasted_iota(jnp.int32, (8, H), 1)
    sub = lax.broadcasted_iota(jnp.int32, (8, H), 0)
    groups = list(groups)
    result = []
    for b in range(16):
        if b in hooks:
            hooks[b]()
        start = 8 * b
        block = (lane >= start) & (lane < start + 8)
        here = groups[b]
        cols = [lane_splat(here, start + s) for s in range(8)]
        swept = jnp.where(block, jnp.where(lane - start == sub, 1.0, 0.0), here)
        scaled = jnp.zeros((8, H), F32)
        for r in range(8):
            pivot = row_splat(cols[r], r)
            inv = 1.0 / pivot
            row = row_splat(swept, r)
            at_r = sub == r
            scaled = jnp.where(at_r, row * lax.rsqrt(pivot), scaled)
            row = row * inv
            swept = jnp.where(at_r, row, swept - cols[r] * row)
            for j in range(r + 1, 8):
                entry = row_splat(cols[j], r) * inv
                cols[j] = jnp.where(at_r, entry, cols[j] - cols[r] * entry)
        result.append(jnp.where(lane <= sub + start, scaled, 0.0))
        rows = [row_splat(swept, s) for s in range(8)]
        for g in range(b + 1, 16):
            terms = [lane_splat(groups[g], start + s) * rows[s] for s in range(8)]
            while len(terms) > 1:
                terms = [terms[i] + terms[i + 1] for i in range(0, len(terms), 2)]
            groups[g] = jnp.where(block, 0.0, groups[g]) - terms[0]
    return result


def place(row):
    core, y, x = row % 2, row // 2 % 4, row // 8
    return core, x * (1 - core) + y * core, y * (1 - core) + x * core


def row_of(core, major, minor):
    x = major * (1 - core) + minor * core
    y = minor * (1 - core) + major * core
    return (x * 4 + y) * 2 + core


def walk_partners():
    row, col = lax.axis_index("row"), lax.axis_index("col")
    core, major, minor = place(row)
    near = [(core, major, (minor + d) % 4) for d in (1, 3)] + [(core, (major + d) % 4, minor) for d in (1, 3)]
    return [(row_of(*entry), col) for entry in near] + [(row + 1 - 2 * core, col)]


class Walk:
    def __init__(self, low1, high1, low2, high2, whole, send, recv):
        self.row, self.col = lax.axis_index("row"), lax.axis_index("col")
        self.core, self.major, self.minor = place(self.row)
        self.parts = low1, high1, low2, high2, whole
        self.send, self.recv = send, recv

    def copies(self, n):
        low1, high1, low2, high2, whole = self.parts
        core, major, minor = self.core, self.major, self.minor

        def copy(ref, device, slot):
            return lambda: pltpu.make_async_remote_copy(
                src_ref=ref,
                dst_ref=ref,
                send_sem=self.send.at[n, slot],
                recv_sem=self.recv.at[n, slot],
                device_id=(device, self.col),
                device_id_type=MESH,
            )

        def ring(low, high, me, device, base):
            after, before = (me + 1) % 4, (me + 3) % 4
            up, down = device(after), device(before)
            return [
                copy(low(n, me), up, base),
                copy(high(n, me), down, base + 1),
                copy(high(n, me), up, base + 2),
                copy(low(n, me), down, base + 3),
                copy(low(n, before), up, base + 4),
                copy(high(n, after), down, base + 5),
            ]

        first = ring(low1, high1, minor, lambda at: row_of(core, major, at), 0)
        second = ring(low2, high2, major, lambda at: row_of(core, at, minor), 6)
        sibling = self.row + 1 - 2 * core
        order = (major, (major + 3) % 4, (major + 1) % 4, (major + 2) % 4)
        across = [copy(whole(n, at), sibling, 12 + i) for i, at in enumerate(order)]
        return first + second + across

    def begin(self, n):
        sent = self.copies(n)
        for i in range(4):
            sent[i]().start()

    def middle(self, n):
        sent = self.copies(n)
        sent[0]().wait_recv()
        sent[4]().start()
        sent[1]().wait_recv()
        sent[5]().start()

    def second(self, n):
        sent = self.copies(n)
        for i in range(2, 6):
            sent[i]().wait_recv()
        for i in (6, 7, 8, 9, 12):
            sent[i]().start()

    def third(self, n):
        sent = self.copies(n)
        sent[6]().wait_recv()
        sent[10]().start()
        sent[7]().wait_recv()
        sent[11]().start()
        sent[8]().wait_recv()
        sent[13]().start()
        sent[9]().wait_recv()
        sent[14]().start()

    def fourth(self, n):
        sent = self.copies(n)
        sent[10]().wait_recv()
        sent[11]().wait_recv()
        sent[15]().start()

    def finish(self, n):
        sent = self.copies(n)
        for i in range(12, 16):
            sent[i]().wait_recv()
        for entry in sent:
            entry().wait_send()


def index_of(i, j):
    return i * (i + 1) // 2 + j


def lanes(k):
    return pl.ds(pl.multiple_of(k * B, B), B)


def factor_kernel(
    strip_ref, panel_ref, rounded_ref, side_ref,
    tiles, strips, lead, inverse, diag, inv_half, mixed, acc,
    fill_send, fill_recv, own_sem, keep_sem, share_send, share_recv, share_own,
    strip_send, strip_recv, lead_send, lead_recv, side_send, side_recv,
):
    row, col = lax.axis_index("row"), lax.axis_index("col")
    core, major, minor = place(row)
    tile = row
    base = row // 4 * 4
    is_source = row % 4 == col
    share = rounded_ref.shape[0] // 4
    at_row = lax.broadcasted_iota(jnp.int32, (2 * B, B), 0)
    at_col = lax.broadcasted_iota(jnp.int32, (2 * B, B), 1)

    def when(condition, action):
        pl.when(condition)(action)

    def span(start, size):
        return pl.ds(pl.multiple_of(start, 8), size)

    lead_walk = Walk(
        lambda n, at: tiles.at[pl.ds(4 * n, 4), span(8 * (core * 16 + major * 4 + at), 8), pl.ds(0, H)],
        lambda n, at: tiles.at[pl.ds(4 * n, 4), span(8 * (core * 16 + major * 4 + at), 8), pl.ds(H, H)],
        lambda n, at: tiles.at[pl.ds(4 * n, 4), span(8 * (core * 16 + at * 4), 16)],
        lambda n, at: tiles.at[pl.ds(4 * n, 4), span(8 * (core * 16 + at * 4) + 16, 16)],
        lambda n, at: tiles.at[pl.ds(4 * n, 4), span(8 * (core * 16 + at * 4), 32)],
        lead_send,
        lead_recv,
    )
    half = share // 2
    side_walk = Walk(
        lambda n, at: side_ref.at[core, major, at, pl.ds(0, half), lanes(n)],
        lambda n, at: side_ref.at[core, major, at, pl.ds(half, half), lanes(n)],
        lambda n, at: side_ref.at[core, at, pl.ds(0, 2), :, lanes(n)],
        lambda n, at: side_ref.at[core, at, pl.ds(2, 2), :, lanes(n)],
        lambda n, at: side_ref.at[core, at, :, :, lanes(n)],
        side_send,
        side_recv,
    )

    mine = [(index_of(row, col + 4 * u), (row < STEPS) & (col + 4 * u <= row)) for u in range(2)]

    def fill(u, to, plane):
        to_core, to_major, to_minor = place(to)
        piece = span(8 * (to_core * 16 + to_major * 4 + to_minor), 8)
        return pltpu.make_async_remote_copy(
            src_ref=strip_ref.at[u, piece],
            dst_ref=tiles.at[mine[u][0], piece],
            send_sem=fill_send.at[u, plane * 32 + to],
            recv_sem=fill_recv.at[mine[u][0] // 4],
            device_id=(to, plane),
            device_id_type=MESH,
        )

    def fill_own(u):
        piece = span(8 * (core * 16 + major * 4 + minor), 8)
        return pltpu.make_async_copy(
            strip_ref.at[u, piece], tiles.at[mine[u][0], piece], fill_recv.at[mine[u][0] // 4]
        )

    def each_fill(action):
        def one(d, carry):
            to, plane = d // 4, d % 4
            for u in range(2):
                when((to != row) | (plane != col), lambda u=u: when(mine[u][1], lambda: action(fill(u, to, plane))))
            return carry

        @pl.when(row < STEPS)
        def _():
            lax.fori_loop(0, 128, one, 0)

    def lead_begin(n):
        here = tiles.at[pl.ds(4 * n, 4), span(8 * (core * 16 + major * 4 + minor), 8)]
        pltpu.make_async_remote_copy(
            src_ref=here,
            dst_ref=here,
            send_sem=own_sem,
            recv_sem=fill_recv.at[n],
            device_id=(base + (row + 1) % 4, col),
            device_id_type=MESH,
        ).wait_recv()
        lead_walk.begin(n)

    def strip_copies(u):
        after, before = (col + 1) % 4, (col + 3) % 4

        def copy(src, dst, to, slot):
            return lambda: pltpu.make_async_remote_copy(
                src_ref=src,
                dst_ref=dst,
                send_sem=strip_send.at[u, slot],
                recv_sem=strip_recv.at[u, slot],
                device_id=(row, to),
                device_id_type=MESH,
            )

        low, high = pl.ds(0, B), pl.ds(B, B)
        near = [
            copy(strip_ref.at[u, part], strips.at[col, u, part], to, slot)
            for slot, (part, to) in enumerate(((low, after), (high, before), (high, after), (low, before)))
        ]
        up, down = strips.at[before, u, low], strips.at[after, u, high]
        return near + [copy(up, up, after, 4), copy(down, down, before, 5)]

    def strip_begin(u):
        for entry in strip_copies(u)[:4]:
            entry().start()

    def strip_pass(u):
        sent = strip_copies(u)
        sent[0]().wait_recv()
        sent[4]().start()
        sent[1]().wait_recv()
        sent[5]().start()

    def strip_finish(u):
        sent = strip_copies(u)
        for i in range(2, 6):
            sent[i]().wait_recv()
        for entry in sent:
            entry().wait_send()

    keep = pltpu.make_async_copy(strip_ref, strips.at[col], keep_sem)

    def share_copy(n, e):
        to = base + e
        to_core, to_major, to_minor = place(to)
        return pltpu.make_async_remote_copy(
            src_ref=rounded_ref.at[pl.ds(e * share, share), lanes(n)],
            dst_ref=side_ref.at[to_core, to_major, to_minor, :, lanes(n)],
            send_sem=share_send.at[n, e],
            recv_sem=share_recv.at[n],
            device_id=(to, col),
            device_id_type=MESH,
        )

    def share_keep(n):
        return pltpu.make_async_copy(
            rounded_ref.at[pl.ds(pl.multiple_of(col * share, share), share), lanes(n)],
            side_ref.at[core, major, minor, :, lanes(n)],
            share_own,
        )

    def solve(n):
        acc[...] = strips[n % 4, n // 4]

        def update(j, carry):
            acc[...] -= dot_bf(rounded_ref[:, lanes(j)], lead[index_of(n, j)], NT)
            return carry

        lax.fori_loop(0, n, update, 0)
        solved = dot_full(acc[...], inverse[n], NT)
        later = (at_row >= B) | (n < tile)
        rounded_ref[:, lanes(n)] = jnp.where(later, solved, 0.0).astype(BF16)

        @pl.when(n % 4 == col)
        def _():
            kept = later | ((n == tile) & (at_col <= at_row))
            panel_ref[n // 4] = jnp.where(kept, solved, 0.0)

        for e in range(4):
            when(is_source & (col != e), lambda e=e: share_copy(n, e).start())
        when(is_source, lambda: share_keep(n).start())

    def side_begin(n):
        when(is_source, lambda: share_keep(n).wait())
        when(jnp.logical_not(is_source), lambda: share_copy(n, (row + 1) % 4).wait_recv())
        side_walk.begin(n)

    def side_finish(n):
        side_walk.finish(n)
        for e in range(4):
            when(is_source & (col != e), lambda e=e: share_copy(n, e).wait_send())

    around = (1, 2, 3)
    partners = walk_partners() + [(base + (row + d) % 4, col) for d in around] + [(row, (col + d) % 4) for d in (1, 3)]
    barrier = pltpu.get_barrier_semaphore()
    for device in partners:
        pl.semaphore_signal(barrier, inc=1, device_id=device, device_id_type=MESH)

    def greet(d, carry):
        to, plane = d // 4, d % 4

        @pl.when((plane <= to) & ((to != row) | (plane != col)))
        def _():
            pl.semaphore_signal(barrier, inc=1, device_id=(to, plane), device_id_type=MESH)

        return carry

    lax.fori_loop(0, 4 * STEPS, greet, 0)
    owner = (row < STEPS) & (col <= row)
    pl.semaphore_wait(barrier, len(partners) + 127 * owner.astype(jnp.int32))

    each_fill(lambda entry: entry.start())
    for u in range(2):
        when(mine[u][1], lambda u=u: fill_own(u).start())
    strip_begin(0)
    keep.start()
    lead_begin(0)
    lead_walk.middle(0)
    lead_walk.second(0)
    lead_walk.third(0)
    lead_walk.fourth(0)
    keep.wait()

    def step(k, carry):
        lead_walk.finish(k)
        when(k >= 2, lambda: side_finish(k - 2))
        at = index_of(k, k)

        def row_tile(j, carry):
            here = index_of(k, j)

            def update(i, carry):
                tiles[here] -= dot_bf(lead[index_of(k, i)], lead[index_of(j, i)], NT)
                return carry

            lax.fori_loop(0, j, update, 0)
            found = dot_full(tiles[here], inverse[j], NT).astype(BF16)
            lead[here] = found
            tiles[at] -= dot_bf(found, found, NT)
            return carry

        lax.fori_loop(0, k, row_tile, 0)

        @pl.when(k == 1)
        def _():
            strip_finish(0)

        @pl.when(k == 5)
        def _():
            strip_finish(1)

        when(k >= 1, lambda: solve(k - 1))

        def half_step(h, carry):
            more, past = k < STEPS - 1, k >= 1

            def at_half(value, condition, action):
                pl.when((h == value) & condition)(action)

            def early():
                at_half(0, more, lambda: lead_begin(k + 1))
                at_half(0, past, lambda: side_begin(k - 1))
                at_half(1, more, lambda: lead_walk.third(k + 1))

            def late():
                at_half(0, more, lambda: lead_walk.middle(k + 1))
                at_half(0, past, lambda: side_walk.middle(k - 1))
                at_half(1, more, lambda: lead_walk.fourth(k + 1))
                at_half(1, past, lambda: side_walk.third(k - 1))

            @pl.when(h == 0)
            def _():
                diag[...] = tiles[at, 0:H, 0:H]

            done = inverse_factor([diag[8 * g : 8 * g + 8, :] for g in range(16)], {5: early, 10: late})
            for g in range(16):
                inv_half[8 * g : 8 * g + 8, :] = done[g]

            @pl.when(h == 0)
            def _():
                when(more, lambda: lead_walk.second(k + 1))
                when(past, lambda: side_walk.second(k - 1))
                when(k == 0, lambda: strip_pass(0))
                when(k == 0, lambda: strip_begin(1))
                when(k == 2, lambda: strip_pass(1))
                first = inv_half[...]
                l21 = dot_full(tiles[at, H:B, 0:H], first, NT)
                diag[...] = tiles[at, H:B, H:B] - dot_full(l21, l21, NT)
                mixed[...] = dot_full(l21, first, NN)
                inverse[k, 0:H, 0:H] = first
                inverse[k, 0:H, H:B] = jnp.zeros((H, H), F32)

            @pl.when(h == 1)
            def _():
                second = inv_half[...]
                inverse[k, H:B, 0:H] = -dot_full(second, mixed[...], NN)
                inverse[k, H:B, H:B] = second
                when(past, lambda: side_walk.fourth(k - 1))

            return carry

        return lax.fori_loop(0, 2, half_step, carry)

    lax.fori_loop(0, STEPS, step, 0)
    last = STEPS - 1
    side_finish(last - 1)
    solve(last)
    side_begin(last)
    side_walk.middle(last)
    side_walk.second(last)
    side_walk.third(last)
    side_walk.fourth(last)
    side_finish(last)
    each_fill(lambda entry: entry.wait_send())


def factor(strip):
    vmem = pl.BlockSpec(memory_space=pltpu.VMEM)
    anywhere = pl.BlockSpec(memory_space=pl.ANY)
    dma = pltpu.SemaphoreType.DMA
    return pl.pallas_call(
        factor_kernel,
        out_shape=(
            jax.ShapeDtypeStruct((2, 2 * B, B), F32),
            jax.ShapeDtypeStruct((2 * B, STEPS * B), BF16),
            jax.ShapeDtypeStruct((2, 4, 4, H, STEPS * B), BF16),
        ),
        in_specs=[anywhere],
        out_specs=(vmem, vmem, anywhere),
        scratch_shapes=[
            pltpu.VMEM((28, B, B), F32),
            pltpu.VMEM((4, 2, 2 * B, B), F32),
            pltpu.VMEM((28, B, B), BF16),
            pltpu.VMEM((STEPS, B, B), F32),
            pltpu.VMEM((H, H), F32),
            pltpu.VMEM((H, H), F32),
            pltpu.VMEM((H, H), F32),
            pltpu.VMEM((2 * B, B), F32),
            dma((2, 128)), dma((STEPS,)), dma, dma, dma((STEPS, 4)), dma((STEPS,)), dma,
            dma((2, 6)), dma((2, 6)), dma((STEPS, 16)), dma((STEPS, 16)), dma((STEPS, 16)), dma((STEPS, 16)),
        ],
        compiler_params=pltpu.CompilerParams(
            has_side_effects=True, collective_id=0, vmem_limit_bytes=48 * 2**20
        ),
    )(strip)


def trailing_kernel(matrix_ref, nugget_ref, panel_ref, rounded_ref, even_ref, odd_ref, out_ref):
    slot = pl.program_id(0)
    tile, col = lax.axis_index("row"), lax.axis_index("col")
    col_tile = slot * 4 + col

    @pl.when(col_tile < STEPS)
    def _():
        out_ref[...] = panel_ref[0]

    @pl.when(col_tile >= STEPS)
    def _():
        side = jnp.concatenate([even_ref[0, 0, 0], odd_ref[0, 0, 0]], axis=0)
        out_ref[...] = matrix_ref[...] - dot_bf(rounded_ref[...], side, NT)
        for s in range(2):
            rows = pl.ds(s * B, B)

            @pl.when(col_tile == s * 32 + tile)
            def _(s=s, rows=rows):
                at_row = lax.broadcasted_iota(jnp.int32, (B, B), 0)
                at_col = lax.broadcasted_iota(jnp.int32, (B, B), 1)
                out_ref[rows, :] += jnp.where(at_row == at_col, nugget_ref[s : s + 1, :], 0.0)

        @pl.when(tile < STEPS)
        def _():
            out_ref[0:B, :] = jnp.zeros((B, B), F32)


def trailing(matrix, nugget, panel, rounded, side):
    rows, cols = matrix.shape
    depth = rounded.shape[1]

    def even(t):
        return (0, t % 8 // 2, 2 * (t % 2) + t // 8, 0, 0)

    def odd(t):
        return (1, 2 * (t % 2) + t // 8, t % 8 // 2, 0, 0)

    return pl.pallas_call(
        trailing_kernel,
        grid=(cols // B,),
        out_shape=jax.ShapeDtypeStruct(matrix.shape, F32),
        in_specs=[
            pl.BlockSpec((rows, B), lambda t: (0, t)),
            pl.BlockSpec((2, B), lambda t: (0, 0)),
            pl.BlockSpec((1, rows, B), lambda t: (jnp.minimum(t, 1), 0, 0)),
            pl.BlockSpec((rows, depth), lambda t: (0, 0)),
            pl.BlockSpec((1, 1, 1, H, depth), even),
            pl.BlockSpec((1, 1, 1, H, depth), odd),
        ],
        out_specs=pl.BlockSpec((rows, B), lambda t: (0, t)),
        compiler_params=pltpu.CompilerParams(vmem_limit_bytes=48 * 2**20),
    )(matrix, nugget, panel, rounded, side, side)


def body(kernel, nugget):
    rows_here = kernel.shape[0]
    tile, col = lax.axis_index("row"), lax.axis_index("col")
    nugget = nugget.reshape(2, B)
    strip = kernel[:, : 2 * B].reshape(rows_here, 2, B).transpose(1, 0, 2)
    col_tile = jnp.arange(2)[:, None, None] * 4 + col
    same = (
        (col_tile == tile)
        & (jnp.arange(rows_here)[None, :, None] == jnp.arange(B)[None, None, :])
    )
    strip = strip + jnp.where(same, nugget[0][None, None, :], 0.0)
    panel, rounded, side = factor(strip)
    return trailing(kernel, nugget, panel, rounded, side)


def solution(mesh):
    return jax.shard_map(
        body,
        mesh=mesh,
        in_specs=(P("row", "col"), P("row")),
        out_specs=P("row", "col"),
        check_vma=False,
    )
```

time: 2170 us -> 280 us (0.13)
  waiting for transfers between devices: 1490 us -> 0 us
  other arithmetic: 422 us -> 0.27 us
  Pallas kernels: 0 us -> 274 us
  local copies, waits for them, and re-layouts: 123 us -> 3.34 us
  matrix products: 61.4 us -> 0 us
  starting transfers between devices: 31.1 us -> 0 us
  between operations: 24 us -> 0.04 us
    psum x14 -> x0, waiting for transfers between devices: 977 us -> none  [broadcast(): return lax.psum(kept, axis)]
    another operation x66 -> x0, other arithmetic: 382 us -> none  [the longest x49 243 us: body(): factor = jnp.linalg.cholesky(diag_tile)]
    all_gather x7 -> x0, waiting for transfers between devices: 337 us -> none  [body(): gathered = lax.all_gather(own_share[None], 'row', axis=0, tiled=True)]
    pallas_call x0 -> x2, Pallas kernels: none -> 274 us  [the longest x1 255 us: factor(): pl.pallas_call(factor_kernel, out_shape=(jax.ShapeDtypeStruct((2, 2 * B,...]
    all_to_all x7 -> x0, waiting for transfers between devices: 177 us -> none  [body(): lax.all_to_all(grouped, 'col', split_axis=1, concat_axis=2, tiled=True)]
    dot_general x7 -> x0, matrix products: 45.7 us -> none  [apply_step(): product = jnp.dot(row_side, col_part.T, preferred_element_type=jnp.float32)]
    reshape x14 -> x2, local copies, waits for them, and re-layouts: 41.9 us -> 1.02 us  [the longest x1 0.69 us: body(): nugget = nugget.reshape(2, B)]
    another operation x71 -> x0, local copies, waits for them, and re-layouts: 29.6 us -> none  [the longest x50 28.2 us: body(): lax.linalg.triangular_solve(factor, panel_strip, left_side=False, lower=T...]
  transfers between devices with their start and end apart: 28 -> 0, of which waited for: 28 -> 0; matrix products, arithmetic and copies ran while one was open for 0% -> 0% of each run, Pallas kernels for 0% -> 0%
where the time goes in v2:
time: 280 us; the launch traced here: 278 us
  Pallas kernels  274 us (98%)
  local copies, waits for them, and re-layouts  3.34 us (1%)
    pallas_call x1, Pallas kernels, factor(): pl.pallas_call(factor_kernel, out_shape=(jax.ShapeDtypeStruct((2, 2 * B,...  255 us
    pallas_call x1, Pallas kernels, trailing(): pl.pallas_call(trailing_kernel, grid=(cols // B,), out_shape=jax.ShapeDty...  19.4 us

profile of v2, /device:TPU:1, one launch (start us, length us, event | category | flops | bytes accessed | tf_op | source)
XLA Modules:
  0.0 277.9 jit_solution(2706161774357056359)
XLA Ops:
  0.0 0.7 slice.8
  0.7 0.7 reshape.33.nugget_ref
  1.4 1.3 slice.7
  2.7 0.3 copy.5
  3.1 0.3 copy.4
  3.4 0.2 bitcast_add_fusion.strip_ref
  3.6 254.8 %shard_map.28 = (f32[2,512,256]{2,1,0:T(8,128)S(1)}, bf16[512,1792]{1,0:T(8,128)(2,1)S(1)}, bf16[2,4,4,128,1792]{4,3,2,1,0:T(8,128)(2,1)}) custom-call(f32[2,512,256]{2,1,0:T(8,128)S(1)} %bitcast_add_fusion.strip_ref), custom_call_target="tpu_custom_call" | custom-call | tf_op jit(solution)/shard_map/pallas_call | solution.py:482
  258.4 19.4 %shard_map.29 = f32[512,4096]{1,0:T(8,128)} custom-call(f32[512,4096]{1,0:T(8,128)} %matrix_ref.1, f32[2,256]{1,0:T(2,128)S(1)} %reshape.33.nugget_ref, f32[2,512,256]{2,1,0:T(8,128)S(1)} %get-tuple-element.8.panel_ref, bf16[512,1792]{1,0:T(8,128)(2,1)S(1)} %get-tuple-element.9.rounded_ref, bf16[2,4,4,128,1792]{4,3,2,1,0:T(8,128)(2,1)} %get-tuple-element.10.even_ref.odd_ref, ...), custom_call_target="tpu_custom_call" | custom-call | tf_op jit(solution)/shard_map/pallas_call | solution.py:546
  (2 shorter events, 0.0 us)

commit v3 on v2

--- a/solution.py
+++ b/solution.py
@@ -15,8 +15,25 @@
 NN = (((1,), (0,)), ((), ()))
 
 
+def pieces(x):
+    high = x.astype(BF16)
+    return high, (x - high.astype(F32)).astype(BF16)
+
+
 def dot_full(a, b, dims):
-    return lax.dot_general(a, b, dims, precision=lax.Precision.HIGHEST, preferred_element_type=F32)
+    a_high, a_low = pieces(a)
+    b_high, b_low = pieces(b)
+    a_axis, b_axis = dims[0][0][0], dims[0][1][0]
+    return dot_bf(
+        jnp.concatenate([a_high, a_high, a_low], axis=a_axis),
+        jnp.concatenate([b_high, b_low, b_high], axis=b_axis),
+        dims,
+    )
+
+
+def dot_inverse(a, terms):
+    high, low = pieces(a)
+    return dot_bf(jnp.concatenate([high, high, low], axis=1), terms, NT)
 
 
 def dot_bf(a, b, dims):
@@ -77,22 +94,15 @@
     return (x * 4 + y) * 2 + core
 
 
-def walk_partners():
-    row, col = lax.axis_index("row"), lax.axis_index("col")
-    core, major, minor = place(row)
-    near = [(core, major, (minor + d) % 4) for d in (1, 3)] + [(core, (major + d) % 4, minor) for d in (1, 3)]
-    return [(row_of(*entry), col) for entry in near] + [(row + 1 - 2 * core, col)]
-
-
 class Walk:
-    def __init__(self, low1, high1, low2, high2, whole, send, recv):
+    def __init__(self, single, low, high, whole, send, recv):
         self.row, self.col = lax.axis_index("row"), lax.axis_index("col")
         self.core, self.major, self.minor = place(self.row)
-        self.parts = low1, high1, low2, high2, whole
+        self.parts = single, low, high, whole
         self.send, self.recv = send, recv
 
     def copies(self, n):
-        low1, high1, low2, high2, whole = self.parts
+        single, low, high, whole = self.parts
         core, major, minor = self.core, self.major, self.minor
 
         def copy(ref, device, slot):
@@ -105,69 +115,76 @@
                 device_id_type=MESH,
             )
 
-        def ring(low, high, me, device, base):
-            after, before = (me + 1) % 4, (me + 3) % 4
-            up, down = device(after), device(before)
-            return [
-                copy(low(n, me), up, base),
-                copy(high(n, me), down, base + 1),
-                copy(high(n, me), up, base + 2),
-                copy(low(n, me), down, base + 3),
-                copy(low(n, before), up, base + 4),
-                copy(high(n, after), down, base + 5),
-            ]
-
-        first = ring(low1, high1, minor, lambda at: row_of(core, major, at), 0)
-        second = ring(low2, high2, major, lambda at: row_of(core, at, minor), 6)
+        first = [
+            copy(single(n, minor), row_of(core, major, (minor + d) % 4), i) for i, d in enumerate((1, 3, 2))
+        ]
+        after, before = (major + 1) % 4, (major + 3) % 4
+        up, down = row_of(core, after, minor), row_of(core, before, minor)
+        second = [
+            copy(low(n, major), up, 3),
+            copy(high(n, major), down, 4),
+            copy(high(n, major), up, 5),
+            copy(low(n, major), down, 6),
+            copy(low(n, before), up, 7),
+            copy(high(n, after), down, 8),
+        ]
         sibling = self.row + 1 - 2 * core
-        order = (major, (major + 3) % 4, (major + 1) % 4, (major + 2) % 4)
-        across = [copy(whole(n, at), sibling, 12 + i) for i, at in enumerate(order)]
-        return first + second + across
+        order = (major, before, after, (major + 2) % 4)
+        return first + second + [copy(whole(n, at), sibling, 9 + i) for i, at in enumerate(order)]
 
     def begin(self, n):
         sent = self.copies(n)
-        for i in range(4):
+        for i in (2, 0, 1):
             sent[i]().start()
-
-    def middle(self, n):
-        sent = self.copies(n)
-        sent[0]().wait_recv()
-        sent[4]().start()
-        sent[1]().wait_recv()
-        sent[5]().start()
 
     def second(self, n):
         sent = self.copies(n)
-        for i in range(2, 6):
+        for i in range(3):
             sent[i]().wait_recv()
-        for i in (6, 7, 8, 9, 12):
+        for i in (3, 4, 5, 6, 9):
             sent[i]().start()
 
     def third(self, n):
         sent = self.copies(n)
+        sent[3]().wait_recv()
+        sent[7]().start()
+        sent[4]().wait_recv()
+        sent[8]().start()
+        sent[5]().wait_recv()
+        sent[10]().start()
         sent[6]().wait_recv()
-        sent[10]().start()
-        sent[7]().wait_recv()
         sent[11]().start()
-        sent[8]().wait_recv()
-        sent[13]().start()
-        sent[9]().wait_recv()
-        sent[14]().start()
 
     def fourth(self, n):
         sent = self.copies(n)
-        sent[10]().wait_recv()
-        sent[11]().wait_recv()
-        sent[15]().start()
+        sent[7]().wait_recv()
+        sent[8]().wait_recv()
+        sent[12]().start()
 
     def finish(self, n):
         sent = self.copies(n)
-        for i in range(12, 16):
+        for i in range(9, 13):
             sent[i]().wait_recv()
         for entry in sent:
             entry().wait_send()
 
 
+GROUP_START = (0, 10)
+GROUP_SIZE = (10, 18)
+FROM_PLANE = ((4, 3, 2, 1), (6, 5, 4, 3))
+
+
+def from_plane_start(group, plane):
+    return GROUP_START[group] + sum(FROM_PLANE[group][:plane])
+
+
+def tile_at(i, j):
+    plane = j % 4
+    early = 4 * j - j * (j - 1) // 2 + i - j
+    late = 10 + 6 * plane - plane * (plane - 1) // 2 + jnp.where(j < 4, i - 4, 3 + i - j)
+    return jnp.where(i < 4, early, late)
+
+
 def index_of(i, j):
     return i * (i + 1) // 2 + j
 
@@ -179,7 +196,7 @@
 def factor_kernel(
     strip_ref, panel_ref, rounded_ref, side_ref,
     tiles, strips, lead, inverse, diag, inv_half, mixed, acc,
-    fill_send, fill_recv, own_sem, keep_sem, share_send, share_recv, share_own,
+    fill_send, fill_recv, onward_send, onward_recv, keep_sem, share_send, share_recv, share_own,
     strip_send, strip_recv, lead_send, lead_recv, side_send, side_recv,
 ):
     row, col = lax.axis_index("row"), lax.axis_index("col")
@@ -192,73 +209,104 @@
     at_col = lax.broadcasted_iota(jnp.int32, (2 * B, B), 1)
 
     def when(condition, action):
-        pl.when(condition)(action)
+        @pl.when(condition)
+        def _():
+            action()
 
     def span(start, size):
         return pl.ds(pl.multiple_of(start, 8), size)
 
+    def group_tiles(g):
+        return pl.ds(GROUP_START[g], GROUP_SIZE[g])
+
     lead_walk = Walk(
-        lambda n, at: tiles.at[pl.ds(4 * n, 4), span(8 * (core * 16 + major * 4 + at), 8), pl.ds(0, H)],
-        lambda n, at: tiles.at[pl.ds(4 * n, 4), span(8 * (core * 16 + major * 4 + at), 8), pl.ds(H, H)],
-        lambda n, at: tiles.at[pl.ds(4 * n, 4), span(8 * (core * 16 + at * 4), 16)],
-        lambda n, at: tiles.at[pl.ds(4 * n, 4), span(8 * (core * 16 + at * 4) + 16, 16)],
-        lambda n, at: tiles.at[pl.ds(4 * n, 4), span(8 * (core * 16 + at * 4), 32)],
+        lambda g, at: tiles.at[group_tiles(g), span(8 * (core * 16 + major * 4 + at), 8)],
+        lambda g, at: tiles.at[group_tiles(g), span(8 * (core * 16 + at * 4), 16)],
+        lambda g, at: tiles.at[group_tiles(g), span(8 * (core * 16 + at * 4) + 16, 16)],
+        lambda g, at: tiles.at[group_tiles(g), span(8 * (core * 16 + at * 4), 32)],
         lead_send,
         lead_recv,
     )
-    half = share // 2
+    half = 2
     side_walk = Walk(
-        lambda n, at: side_ref.at[core, major, at, pl.ds(0, half), lanes(n)],
-        lambda n, at: side_ref.at[core, major, at, pl.ds(half, half), lanes(n)],
-        lambda n, at: side_ref.at[core, at, pl.ds(0, 2), :, lanes(n)],
-        lambda n, at: side_ref.at[core, at, pl.ds(2, 2), :, lanes(n)],
+        lambda n, at: side_ref.at[core, major, at, :, lanes(n)],
+        lambda n, at: side_ref.at[core, at, pl.ds(0, half), :, lanes(n)],
+        lambda n, at: side_ref.at[core, at, pl.ds(half, half), :, lanes(n)],
         lambda n, at: side_ref.at[core, at, :, :, lanes(n)],
         side_send,
         side_recv,
     )
 
-    mine = [(index_of(row, col + 4 * u), (row < STEPS) & (col + 4 * u <= row)) for u in range(2)]
-
-    def fill(u, to, plane):
+    piece = span(8 * (core * 16 + major * 4 + minor), 8)
+    mine = []
+    for u in range(2):
+        mine.append((tile_at(row, col + 4 * u), (row >= 4).astype(jnp.int32), (row < STEPS) & (col + 4 * u <= row)))
+
+    def fill(u, to):
         to_core, to_major, to_minor = place(to)
-        piece = span(8 * (to_core * 16 + to_major * 4 + to_minor), 8)
+        there = span(8 * (to_core * 16 + to_major * 4 + to_minor), 8)
         return pltpu.make_async_remote_copy(
-            src_ref=strip_ref.at[u, piece],
-            dst_ref=tiles.at[mine[u][0], piece],
-            send_sem=fill_send.at[u, plane * 32 + to],
-            recv_sem=fill_recv.at[mine[u][0] // 4],
-            device_id=(to, plane),
+            src_ref=strip_ref.at[u, there],
+            dst_ref=tiles.at[mine[u][0], there],
+            send_sem=fill_send.at[u, to],
+            recv_sem=fill_recv.at[mine[u][1]],
+            device_id=(to, col),
             device_id_type=MESH,
         )
 
     def fill_own(u):
-        piece = span(8 * (core * 16 + major * 4 + minor), 8)
         return pltpu.make_async_copy(
-            strip_ref.at[u, piece], tiles.at[mine[u][0], piece], fill_recv.at[mine[u][0] // 4]
+            strip_ref.at[u, piece], tiles.at[mine[u][0], piece], fill_recv.at[mine[u][1]]
         )
 
     def each_fill(action):
-        def one(d, carry):
-            to, plane = d // 4, d % 4
+        def one(to, carry):
             for u in range(2):
-                when((to != row) | (plane != col), lambda u=u: when(mine[u][1], lambda: action(fill(u, to, plane))))
+                when((to != row) & mine[u][2], lambda u=u: action(fill(u, to)))
             return carry
 
-        @pl.when(row < STEPS)
-        def _():
-            lax.fori_loop(0, 128, one, 0)
-
-    def lead_begin(n):
-        here = tiles.at[pl.ds(4 * n, 4), span(8 * (core * 16 + major * 4 + minor), 8)]
-        pltpu.make_async_remote_copy(
-            src_ref=here,
-            dst_ref=here,
-            send_sem=own_sem,
-            recv_sem=fill_recv.at[n],
-            device_id=(base + (row + 1) % 4, col),
+        when(row < STEPS, lambda: lax.fori_loop(0, 32, one, 0))
+
+    def onward(g, plane, to):
+        block = tiles.at[pl.ds(from_plane_start(g, plane), FROM_PLANE[g][plane]), piece]
+        return pltpu.make_async_remote_copy(
+            src_ref=block,
+            dst_ref=block,
+            send_sem=onward_send.at[g, to],
+            recv_sem=onward_recv.at[g, plane],
+            device_id=(row, to),
             device_id_type=MESH,
-        ).wait_recv()
-        lead_walk.begin(n)
+        )
+
+    def onward_begin(g):
+        for plane in range(4):
+            @pl.when(col == plane)
+            def _(plane=plane):
+                block = tiles.at[pl.ds(from_plane_start(g, plane), FROM_PLANE[g][plane]), piece]
+                pltpu.make_async_remote_copy(
+                    src_ref=block,
+                    dst_ref=block,
+                    send_sem=onward_send.at[g, plane],
+                    recv_sem=fill_recv.at[g],
+                    device_id=(base + (row + 1) % 4, col),
+                    device_id_type=MESH,
+                ).wait_recv()
+                for to in range(4):
+                    if to != plane:
+                        onward(g, plane, to).start()
+
+    def lead_begin(g):
+        for plane in range(4):
+            when(col != plane, lambda plane=plane: onward(g, plane, (plane + 1) % 4).wait_recv())
+        lead_walk.begin(g)
+
+    def onward_finish(g):
+        for plane in range(4):
+            @pl.when(col == plane)
+            def _(plane=plane):
+                for to in range(4):
+                    if to != plane:
+                        onward(g, plane, to).wait_send()
 
     def strip_copies(u):
         after, before = (col + 1) % 4, (col + 3) % 4
@@ -320,6 +368,11 @@
             share_own,
         )
 
+    def put_inverse(k, at_r, at_c, value):
+        high, low = pieces(value)
+        for start, part in ((0, high), (B, low), (2 * B, high)):
+            inverse[k, at_r : at_r + H, start + at_c : start + at_c + H] = part
+
     def solve(n):
         acc[...] = strips[n % 4, n // 4]
 
@@ -328,7 +381,7 @@
             return carry
 
         lax.fori_loop(0, n, update, 0)
-        solved = dot_full(acc[...], inverse[n], NT)
+        solved = dot_inverse(acc[...], inverse[n])
         later = (at_row >= B) | (n < tile)
         rounded_ref[:, lanes(n)] = jnp.where(later, solved, 0.0).astype(BF16)
 
@@ -351,52 +404,51 @@
         for e in range(4):
             when(is_source & (col != e), lambda e=e: share_copy(n, e).wait_send())
 
-    around = (1, 2, 3)
-    partners = walk_partners() + [(base + (row + d) % 4, col) for d in around] + [(row, (col + d) % 4) for d in (1, 3)]
+    partners = [(row_of(core, major, (minor + d) % 4), col) for d in (1, 2, 3)]
+    partners += [(row_of(core, (major + d) % 4, minor), col) for d in (1, 3)]
+    partners += [(row + 1 - 2 * core, col)]
+    partners += [(base + (row + d) % 4, col) for d in (1, 2, 3)]
+    partners += [(row, (col + d) % 4) for d in (1, 2, 3)]
     barrier = pltpu.get_barrier_semaphore()
     for device in partners:
         pl.semaphore_signal(barrier, inc=1, device_id=device, device_id_type=MESH)
-
-    def greet(d, carry):
-        to, plane = d // 4, d % 4
-
-        @pl.when((plane <= to) & ((to != row) | (plane != col)))
-        def _():
-            pl.semaphore_signal(barrier, inc=1, device_id=(to, plane), device_id_type=MESH)
-
-        return carry
-
-    lax.fori_loop(0, 4 * STEPS, greet, 0)
+    for to in range(STEPS):
+        @pl.when((col <= to) & (row != to))
+        def _(to=to):
+            pl.semaphore_signal(barrier, inc=1, device_id=(to, col), device_id_type=MESH)
     owner = (row < STEPS) & (col <= row)
-    pl.semaphore_wait(barrier, len(partners) + 127 * owner.astype(jnp.int32))
+    pl.semaphore_wait(barrier, len(partners) + 31 * owner.astype(jnp.int32))
 
     each_fill(lambda entry: entry.start())
     for u in range(2):
-        when(mine[u][1], lambda u=u: fill_own(u).start())
+        when(mine[u][2], lambda u=u: fill_own(u).start())
+    onward_begin(0)
     strip_begin(0)
     keep.start()
     lead_begin(0)
-    lead_walk.middle(0)
+    onward_begin(1)
     lead_walk.second(0)
     lead_walk.third(0)
     lead_walk.fourth(0)
+    lead_walk.finish(0)
+    onward_finish(0)
     keep.wait()
 
     def step(k, carry):
-        lead_walk.finish(k)
-        when(k >= 2, lambda: side_finish(k - 2))
-        at = index_of(k, k)
+        when(k == 4, lambda: lead_walk.finish(1))
+        when(k == 4, lambda: onward_finish(1))
+        at = tile_at(k, k)
 
         def row_tile(j, carry):
-            here = index_of(k, j)
+            here = tile_at(k, j)
 
             def update(i, carry):
                 tiles[here] -= dot_bf(lead[index_of(k, i)], lead[index_of(j, i)], NT)
                 return carry
 
             lax.fori_loop(0, j, update, 0)
-            found = dot_full(tiles[here], inverse[j], NT).astype(BF16)
-            lead[here] = found
+            found = dot_inverse(tiles[here], inverse[j]).astype(BF16)
+            lead[index_of(k, j)] = found
             tiles[at] -= dot_bf(found, found, NT)
             return carry
 
@@ -413,50 +465,49 @@
         when(k >= 1, lambda: solve(k - 1))
 
         def half_step(h, carry):
-            more, past = k < STEPS - 1, k >= 1
-
             def at_half(value, condition, action):
                 pl.when((h == value) & condition)(action)
 
             def early():
-                at_half(0, more, lambda: lead_begin(k + 1))
-                at_half(0, past, lambda: side_begin(k - 1))
-                at_half(1, more, lambda: lead_walk.third(k + 1))
+                at_half(0, k == 0, lambda: lead_begin(1))
+
+            def middle():
+                at_half(0, k >= 3, lambda: side_finish(k - 3))
+                at_half(0, k >= 2, lambda: side_walk.third(k - 2))
+                at_half(0, k >= 1, lambda: side_begin(k - 1))
+                at_half(0, k == 0, lambda: strip_pass(0))
+                at_half(1, k >= 2, lambda: side_walk.fourth(k - 2))
+                at_half(1, k >= 1, lambda: side_walk.second(k - 1))
 
             def late():
-                at_half(0, more, lambda: lead_walk.middle(k + 1))
-                at_half(0, past, lambda: side_walk.middle(k - 1))
-                at_half(1, more, lambda: lead_walk.fourth(k + 1))
-                at_half(1, past, lambda: side_walk.third(k - 1))
+                at_half(0, k == 0, lambda: lead_walk.second(1))
 
             @pl.when(h == 0)
             def _():
                 diag[...] = tiles[at, 0:H, 0:H]
 
-            done = inverse_factor([diag[8 * g : 8 * g + 8, :] for g in range(16)], {5: early, 10: late})
+            done = inverse_factor([diag[8 * g : 8 * g + 8, :] for g in range(16)], {4: early, 10: middle, 14: late})
             for g in range(16):
                 inv_half[8 * g : 8 * g + 8, :] = done[g]
 
             @pl.when(h == 0)
             def _():
-                when(more, lambda: lead_walk.second(k + 1))
-                when(past, lambda: side_walk.second(k - 1))
-                when(k == 0, lambda: strip_pass(0))
-                when(k == 0, lambda: strip_begin(1))
-                when(k == 2, lambda: strip_pass(1))
+                when(k == 1, lambda: lead_walk.third(1))
+                when(k == 1, lambda: strip_begin(1))
+                when(k == 2, lambda: lead_walk.fourth(1))
+                when(k == 3, lambda: strip_pass(1))
                 first = inv_half[...]
                 l21 = dot_full(tiles[at, H:B, 0:H], first, NT)
                 diag[...] = tiles[at, H:B, H:B] - dot_full(l21, l21, NT)
                 mixed[...] = dot_full(l21, first, NN)
-                inverse[k, 0:H, 0:H] = first
-                inverse[k, 0:H, H:B] = jnp.zeros((H, H), F32)
+                put_inverse(k, 0, 0, first)
+                put_inverse(k, 0, H, jnp.zeros((H, H), F32))
 
             @pl.when(h == 1)
             def _():
                 second = inv_half[...]
-                inverse[k, H:B, 0:H] = -dot_full(second, mixed[...], NN)
-                inverse[k, H:B, H:B] = second
-                when(past, lambda: side_walk.fourth(k - 1))
+                put_inverse(k, H, 0, -dot_full(second, mixed[...], NN))
+                put_inverse(k, H, H, second)
 
             return carry
 
@@ -464,11 +515,13 @@
 
     lax.fori_loop(0, STEPS, step, 0)
     last = STEPS - 1
+    solve(last)
+    side_finish(last - 2)
+    side_walk.third(last - 1)
+    side_begin(last)
+    side_walk.fourth(last - 1)
+    side_walk.second(last)
     side_finish(last - 1)
-    solve(last)
-    side_begin(last)
-    side_walk.middle(last)
-    side_walk.second(last)
     side_walk.third(last)
     side_walk.fourth(last)
     side_finish(last)
@@ -492,13 +545,13 @@
             pltpu.VMEM((28, B, B), F32),
             pltpu.VMEM((4, 2, 2 * B, B), F32),
             pltpu.VMEM((28, B, B), BF16),
-            pltpu.VMEM((STEPS, B, B), F32),
+            pltpu.VMEM((STEPS, B, 3 * B), BF16),
             pltpu.VMEM((H, H), F32),
             pltpu.VMEM((H, H), F32),
             pltpu.VMEM((H, H), F32),
             pltpu.VMEM((2 * B, B), F32),
-            dma((2, 128)), dma((STEPS,)), dma, dma, dma((STEPS, 4)), dma((STEPS,)), dma,
-            dma((2, 6)), dma((2, 6)), dma((STEPS, 16)), dma((STEPS, 16)), dma((STEPS, 16)), dma((STEPS, 16)),
+            dma((2, 32)), dma((2,)), dma((2, 4)), dma((2, 4)), dma, dma((STEPS, 4)), dma((STEPS,)), dma,
+            dma((2, 6)), dma((2, 6)), dma((2, 13)), dma((2, 13)), dma((STEPS, 13)), dma((STEPS, 13)),
         ],
         compiler_params=pltpu.CompilerParams(
             has_side_effects=True, collective_id=0, vmem_limit_bytes=48 * 2**20

time: 280 us -> 179 us (0.64)
  Pallas kernels: 274 us -> 175 us
    pallas_call x1, Pallas kernels: 255 us -> 155 us  [factor(): pl.pallas_call(factor_kernel, out_shape=(jax.ShapeDtypeStruct((2, 2 * B,...]
where the time goes in v3:
time: 179 us; the launch traced here: 178 us
  Pallas kernels  175 us (98%)
  local copies, waits for them, and re-layouts  3.34 us (2%)
    pallas_call x1, Pallas kernels, factor(): pl.pallas_call(factor_kernel, out_shape=(jax.ShapeDtypeStruct((2, 2 * B,...  155 us
    pallas_call x1, Pallas kernels, trailing(): pl.pallas_call(trailing_kernel, grid=(cols // B,), out_shape=jax.ShapeDty...  19.4 us

profile of v3, /device:TPU:1, one launch (start us, length us, event | category | flops | bytes accessed | tf_op | source)
XLA Modules:
  0.0 178.3 jit_solution(16037806845033640194)
XLA Ops:
  0.0 0.7 slice.8
  0.7 0.7 reshape.33.nugget_ref
  1.4 1.3 slice.7
  2.7 0.3 copy.5
  3.1 0.3 copy.4
  3.4 0.2 bitcast_add_fusion.strip_ref
  3.6 155.2 %shard_map.28 = (f32[2,512,256]{2,1,0:T(8,128)S(1)}, bf16[512,1792]{1,0:T(8,128)(2,1)S(1)}, bf16[2,4,4,128,1792]{4,3,2,1,0:T(8,128)(2,1)}) custom-call(f32[2,512,256]{2,1,0:T(8,128)S(1)} %bitcast_add_fusion.strip_ref), custom_call_target="tpu_custom_call" | custom-call | tf_op jit(solution)/shard_map/pallas_call | solution.py:535
  158.9 19.4 %shard_map.29 = f32[512,4096]{1,0:T(8,128)} custom-call(f32[512,4096]{1,0:T(8,128)} %matrix_ref.1, f32[2,256]{1,0:T(2,128)S(1)} %reshape.33.nugget_ref, f32[2,512,256]{2,1,0:T(8,128)S(1)} %get-tuple-element.8.panel_ref, bf16[512,1792]{1,0:T(8,128)(2,1)S(1)} %get-tuple-element.9.rounded_ref, bf16[2,4,4,128,1792]{4,3,2,1,0:T(8,128)(2,1)} %get-tuple-element.10.even_ref.odd_ref, ...), custom_call_target="tpu_custom_call" | custom-call | tf_op jit(solution)/shard_map/pallas_call | solution.py:599
  (2 shorter events, 0.0 us)

commit v4 on v3

--- a/solution.py
+++ b/solution.py
@@ -8,6 +8,7 @@
 B = 256
 H = 128
 STEPS = 7
+WIDE = 4
 F32 = jnp.float32
 BF16 = jnp.bfloat16
 MESH = pl.DeviceIdType.MESH
@@ -61,25 +62,41 @@
         here = groups[b]
         cols = [lane_splat(here, start + s) for s in range(8)]
         swept = jnp.where(block, jnp.where(lane - start == sub, 1.0, 0.0), here)
-        scaled = jnp.zeros((8, H), F32)
-        for r in range(8):
-            pivot = row_splat(cols[r], r)
-            inv = 1.0 / pivot
-            row = row_splat(swept, r)
-            at_r = sub == r
-            scaled = jnp.where(at_r, row * lax.rsqrt(pivot), scaled)
-            row = row * inv
-            swept = jnp.where(at_r, row, swept - cols[r] * row)
-            for j in range(r + 1, 8):
-                entry = row_splat(cols[j], r) * inv
-                cols[j] = jnp.where(at_r, entry, cols[j] - cols[r] * entry)
-        result.append(jnp.where(lane <= sub + start, scaled, 0.0))
+        scaled = pivots = jnp.ones((8, H), F32)
+        for r in range(0, 8, 2):
+            a, c, d = row_splat(cols[r], r), row_splat(cols[r + 1], r), row_splat(cols[r + 1], r + 1)
+            det = a * d - c * c
+            inv = 1.0 / det
+            at_0, at_1 = sub == r, sub == r + 1
+            inv_a = 1.0 / a
+
+            def sweep(x):
+                u, v = row_splat(x, r), row_splat(x, r + 1)
+                first, second = (d * u - c * v) * inv, (a * v - c * u) * inv
+                rest = x - (cols[r] * first + cols[r + 1] * second)
+                return jnp.where(at_0, first, jnp.where(at_1, second, rest)), u, v
+
+            new, u, v = sweep(swept)
+            scaled = jnp.where(at_0, u, jnp.where(at_1, v - (c * inv_a) * u, scaled))
+            pivots = jnp.where(at_0, a, jnp.where(at_1, det * inv_a, pivots))
+            swept = new
+            for j in range(r + 2, 8):
+                cols[j] = sweep(cols[j])[0]
+        result.append(jnp.where(lane <= sub + start, scaled * lax.rsqrt(pivots), 0.0))
         rows = [row_splat(swept, s) for s in range(8)]
-        for g in range(b + 1, 16):
+        near = min(b + 1, 15)
+        if near < 15:
+            zero = jnp.zeros((8, H), F32)
+            spread = jnp.concatenate([swept if g == b else zero for g in range(16)], axis=0)
+            far = dot_full(jnp.concatenate(groups[near + 1 :], axis=0), spread, NN)
+        for g in range(b + 1, near + 1):
             terms = [lane_splat(groups[g], start + s) * rows[s] for s in range(8)]
             while len(terms) > 1:
                 terms = [terms[i] + terms[i + 1] for i in range(0, len(terms), 2)]
             groups[g] = jnp.where(block, 0.0, groups[g]) - terms[0]
+        for g in range(near + 1, 16):
+            at = 8 * (g - near - 1)
+            groups[g] = jnp.where(block, 0.0, groups[g]) - far[at : at + 8]
     return result
 
 
@@ -95,11 +112,11 @@
 
 
 class Walk:
-    def __init__(self, single, low, high, whole, send, recv):
+    def __init__(self, single, low, high, whole, send, recv, direct=False):
         self.row, self.col = lax.axis_index("row"), lax.axis_index("col")
         self.core, self.major, self.minor = place(self.row)
         self.parts = single, low, high, whole
-        self.send, self.recv = send, recv
+        self.send, self.recv, self.direct = send, recv, direct
 
     def copies(self, n):
         single, low, high, whole = self.parts
@@ -128,9 +145,13 @@
             copy(low(n, before), up, 7),
             copy(high(n, after), down, 8),
         ]
+        if self.direct:
+            block = whole(n, major)
+            second = [copy(block, row_of(core, (major + d) % 4, minor), 3 + i) for i, d in enumerate((1, 3, 2))]
         sibling = self.row + 1 - 2 * core
         order = (major, before, after, (major + 2) % 4)
-        return first + second + [copy(whole(n, at), sibling, 9 + i) for i, at in enumerate(order)]
+        start = 3 + len(second)
+        return first + second + [copy(whole(n, at), sibling, start + i) for i, at in enumerate(order)]
 
     def begin(self, n):
         sent = self.copies(n)
@@ -141,11 +162,16 @@
         sent = self.copies(n)
         for i in range(3):
             sent[i]().wait_recv()
-        for i in (3, 4, 5, 6, 9):
+        for i in (5, 3, 4, 6) if self.direct else (3, 4, 5, 6, 9):
             sent[i]().start()
 
     def third(self, n):
         sent = self.copies(n)
+        if self.direct:
+            for i in range(3, 6):
+                sent[i]().wait_recv()
+                sent[i + 4]().start()
+            return
         sent[3]().wait_recv()
         sent[7]().start()
         sent[4]().wait_recv()
@@ -163,8 +189,8 @@
 
     def finish(self, n):
         sent = self.copies(n)
-        for i in range(9, 13):
-            sent[i]().wait_recv()
+        for entry in sent[-4:]:
+            entry().wait_recv()
         for entry in sent:
             entry().wait_send()
 
@@ -194,7 +220,7 @@
 
 
 def factor_kernel(
-    strip_ref, panel_ref, rounded_ref, side_ref,
+    matrix_ref, nugget_ref, panel_ref, rounded_ref, side_ref,
     tiles, strips, lead, inverse, diag, inv_half, mixed, acc,
     fill_send, fill_recv, onward_send, onward_recv, keep_sem, share_send, share_recv, share_own,
     strip_send, strip_recv, lead_send, lead_recv, side_send, side_recv,
@@ -246,7 +272,7 @@
         to_core, to_major, to_minor = place(to)
         there = span(8 * (to_core * 16 + to_major * 4 + to_minor), 8)
         return pltpu.make_async_remote_copy(
-            src_ref=strip_ref.at[u, there],
+            src_ref=strips.at[col, u, there],
             dst_ref=tiles.at[mine[u][0], there],
             send_sem=fill_send.at[u, to],
             recv_sem=fill_recv.at[mine[u][1]],
@@ -256,7 +282,7 @@
 
     def fill_own(u):
         return pltpu.make_async_copy(
-            strip_ref.at[u, piece], tiles.at[mine[u][0], piece], fill_recv.at[mine[u][1]]
+            strips.at[col, u, piece], tiles.at[mine[u][0], piece], fill_recv.at[mine[u][1]]
         )
 
     def each_fill(action):
@@ -323,7 +349,7 @@
 
         low, high = pl.ds(0, B), pl.ds(B, B)
         near = [
-            copy(strip_ref.at[u, part], strips.at[col, u, part], to, slot)
+            copy(strips.at[col, u, part], strips.at[col, u, part], to, slot)
             for slot, (part, to) in enumerate(((low, after), (high, before), (high, after), (low, before)))
         ]
         up, down = strips.at[before, u, low], strips.at[after, u, high]
@@ -347,7 +373,8 @@
         for entry in sent:
             entry().wait_send()
 
-    keep = pltpu.make_async_copy(strip_ref, strips.at[col], keep_sem)
+    def keep(u):
+        return pltpu.make_async_copy(matrix_ref.at[:, pl.ds(u * B, B)], strips.at[col, u], keep_sem.at[u])
 
     def share_copy(n, e):
         to = base + e
@@ -404,8 +431,11 @@
         for e in range(4):
             when(is_source & (col != e), lambda e=e: share_copy(n, e).wait_send())
 
+    for u in range(2):
+        keep(u).start()
+
     partners = [(row_of(core, major, (minor + d) % 4), col) for d in (1, 2, 3)]
-    partners += [(row_of(core, (major + d) % 4, minor), col) for d in (1, 3)]
+    partners += [(row_of(core, (major + d) % 4, minor), col) for d in (1, 2, 3)]
     partners += [(row + 1 - 2 * core, col)]
     partners += [(base + (row + d) % 4, col) for d in (1, 2, 3)]
     partners += [(row, (col + d) % 4) for d in (1, 2, 3)]
@@ -416,6 +446,13 @@
         @pl.when((col <= to) & (row != to))
         def _(to=to):
             pl.semaphore_signal(barrier, inc=1, device_id=(to, col), device_id_type=MESH)
+    for u in range(2):
+        keep(u).wait()
+
+        @pl.when(col + 4 * u == row)
+        def _(u=u):
+            strips[col, u, 0:B] += jnp.where(at_row[0:B] == at_col[0:B], nugget_ref[:, 0:B], 0.0)
+
     owner = (row < STEPS) & (col <= row)
     pl.semaphore_wait(barrier, len(partners) + 31 * owner.astype(jnp.int32))
 
@@ -424,7 +461,6 @@
         when(mine[u][2], lambda u=u: fill_own(u).start())
     onward_begin(0)
     strip_begin(0)
-    keep.start()
     lead_begin(0)
     onward_begin(1)
     lead_walk.second(0)
@@ -432,7 +468,6 @@
     lead_walk.fourth(0)
     lead_walk.finish(0)
     onward_finish(0)
-    keep.wait()
 
     def step(k, carry):
         when(k == 4, lambda: lead_walk.finish(1))
@@ -469,32 +504,30 @@
                 pl.when((h == value) & condition)(action)
 
             def early():
+                at_half(0, k >= 3, lambda: side_walk.fourth(k - 3))
                 at_half(0, k == 0, lambda: lead_begin(1))
-
-            def middle():
-                at_half(0, k >= 3, lambda: side_finish(k - 3))
-                at_half(0, k >= 2, lambda: side_walk.third(k - 2))
+                at_half(1, k >= 3, lambda: side_finish(k - 3))
+                at_half(1, k >= 2, lambda: side_walk.third(k - 2))
+                at_half(1, k == 0, lambda: lead_walk.second(1))
+
+            def late():
                 at_half(0, k >= 1, lambda: side_begin(k - 1))
                 at_half(0, k == 0, lambda: strip_pass(0))
-                at_half(1, k >= 2, lambda: side_walk.fourth(k - 2))
                 at_half(1, k >= 1, lambda: side_walk.second(k - 1))
-
-            def late():
-                at_half(0, k == 0, lambda: lead_walk.second(1))
 
             @pl.when(h == 0)
             def _():
                 diag[...] = tiles[at, 0:H, 0:H]
 
-            done = inverse_factor([diag[8 * g : 8 * g + 8, :] for g in range(16)], {4: early, 10: middle, 14: late})
+            done = inverse_factor([diag[8 * g : 8 * g + 8, :] for g in range(16)], {3: early, 11: late})
             for g in range(16):
                 inv_half[8 * g : 8 * g + 8, :] = done[g]
 
             @pl.when(h == 0)
             def _():
                 when(k == 1, lambda: lead_walk.third(1))
+                when(k == 2, lambda: lead_walk.fourth(1))
                 when(k == 1, lambda: strip_begin(1))
-                when(k == 2, lambda: lead_walk.fourth(1))
                 when(k == 3, lambda: strip_pass(1))
                 first = inv_half[...]
                 l21 = dot_full(tiles[at, H:B, 0:H], first, NT)
@@ -516,9 +549,10 @@
     lax.fori_loop(0, STEPS, step, 0)
     last = STEPS - 1
     solve(last)
-    side_finish(last - 2)
+    side_walk.fourth(last - 2)
     side_walk.third(last - 1)
     side_begin(last)
+    side_finish(last - 2)
     side_walk.fourth(last - 1)
     side_walk.second(last)
     side_finish(last - 1)
@@ -528,7 +562,7 @@
     each_fill(lambda entry: entry.wait_send())
 
 
-def factor(strip):
+def factor(matrix, nugget):
     vmem = pl.BlockSpec(memory_space=pltpu.VMEM)
     anywhere = pl.BlockSpec(memory_space=pl.ANY)
     dma = pltpu.SemaphoreType.DMA
@@ -539,7 +573,7 @@
             jax.ShapeDtypeStruct((2 * B, STEPS * B), BF16),
             jax.ShapeDtypeStruct((2, 4, 4, H, STEPS * B), BF16),
         ),
-        in_specs=[anywhere],
+        in_specs=[anywhere, vmem],
         out_specs=(vmem, vmem, anywhere),
         scratch_shapes=[
             pltpu.VMEM((28, B, B), F32),
@@ -550,81 +584,84 @@
             pltpu.VMEM((H, H), F32),
             pltpu.VMEM((H, H), F32),
             pltpu.VMEM((2 * B, B), F32),
-            dma((2, 32)), dma((2,)), dma((2, 4)), dma((2, 4)), dma, dma((STEPS, 4)), dma((STEPS,)), dma,
+            dma((2, 32)), dma((2,)), dma((2, 4)), dma((2, 4)), dma((2,)), dma((STEPS, 4)), dma((STEPS,)), dma,
             dma((2, 6)), dma((2, 6)), dma((2, 13)), dma((2, 13)), dma((STEPS, 13)), dma((STEPS, 13)),
         ],
         compiler_params=pltpu.CompilerParams(
             has_side_effects=True, collective_id=0, vmem_limit_bytes=48 * 2**20
         ),
-    )(strip)
-
-
-def trailing_kernel(matrix_ref, nugget_ref, panel_ref, rounded_ref, even_ref, odd_ref, out_ref):
-    slot = pl.program_id(0)
+    )(matrix, nugget)
+
+
+def trailing_kernel(matrix_ref, nugget_ref, panel_ref, rounded_ref, *refs):
+    out_ref = refs[-1]
     tile, col = lax.axis_index("row"), lax.axis_index("col")
-    col_tile = slot * 4 + col
-
-    @pl.when(col_tile < STEPS)
-    def _():
-        out_ref[...] = panel_ref[0]
-
-    @pl.when(col_tile >= STEPS)
-    def _():
-        side = jnp.concatenate([even_ref[0, 0, 0], odd_ref[0, 0, 0]], axis=0)
-        out_ref[...] = matrix_ref[...] - dot_bf(rounded_ref[...], side, NT)
-        for s in range(2):
-            rows = pl.ds(s * B, B)
-
-            @pl.when(col_tile == s * 32 + tile)
-            def _(s=s, rows=rows):
-                at_row = lax.broadcasted_iota(jnp.int32, (B, B), 0)
-                at_col = lax.broadcasted_iota(jnp.int32, (B, B), 1)
-                out_ref[rows, :] += jnp.where(at_row == at_col, nugget_ref[s : s + 1, :], 0.0)
-
-        @pl.when(tile < STEPS)
-        def _():
-            out_ref[0:B, :] = jnp.zeros((B, B), F32)
+    for u in range(WIDE):
+        even_ref, odd_ref = refs[2 * u], refs[2 * u + 1]
+        slot = pl.program_id(0) * WIDE + u
+        col_tile = slot * 4 + col
+        here = slice(u * B, (u + 1) * B)
+
+        @pl.when(col_tile < STEPS)
+        def _(slot=slot, here=here):
+            out_ref[:, here] = panel_ref[jnp.minimum(slot, 1)]
+
+        @pl.when(col_tile >= STEPS)
+        def _(even_ref=even_ref, odd_ref=odd_ref, col_tile=col_tile, here=here):
+            side = jnp.concatenate([even_ref[0, 0, 0], odd_ref[0, 0, 0]], axis=0)
+            out_ref[:, here] = matrix_ref[:, here] - dot_bf(rounded_ref[...], side, NT)
+            for s in range(2):
+                @pl.when(col_tile == s * 32 + tile)
+                def _(s=s):
+                    rows = slice(s * B, (s + 1) * B)
+                    at_row = lax.broadcasted_iota(jnp.int32, (B, B), 0)
+                    at_col = lax.broadcasted_iota(jnp.int32, (B, B), 1)
+                    out_ref[rows, here] += jnp.where(at_row == at_col, nugget_ref[:, rows], 0.0)
+
+            @pl.when(tile < STEPS)
+            def _():
+                out_ref[0:B, here] = jnp.zeros((B, B), F32)
 
 
 def trailing(matrix, nugget, panel, rounded, side):
     rows, cols = matrix.shape
     depth = rounded.shape[1]
 
-    def even(t):
-        return (0, t % 8 // 2, 2 * (t % 2) + t // 8, 0, 0)
-
-    def odd(t):
-        return (1, 2 * (t % 2) + t // 8, t % 8 // 2, 0, 0)
-
+    def even(u):
+        def at(g):
+            t = g * WIDE + u
+            return (0, t % 8 // 2, 2 * (t % 2) + t // 8, 0, 0)
+
+        return at
+
+    def odd(u):
+        def at(g):
+            t = g * WIDE + u
+            return (1, 2 * (t % 2) + t // 8, t % 8 // 2, 0, 0)
+
+        return at
+
+    blocks = []
+    for u in range(WIDE):
+        blocks += [pl.BlockSpec((1, 1, 1, H, depth), even(u)), pl.BlockSpec((1, 1, 1, H, depth), odd(u))]
     return pl.pallas_call(
         trailing_kernel,
-        grid=(cols // B,),
+        grid=(cols // (WIDE * B),),
         out_shape=jax.ShapeDtypeStruct(matrix.shape, F32),
         in_specs=[
-            pl.BlockSpec((rows, B), lambda t: (0, t)),
-            pl.BlockSpec((2, B), lambda t: (0, 0)),
-            pl.BlockSpec((1, rows, B), lambda t: (jnp.minimum(t, 1), 0, 0)),
+            pl.BlockSpec((rows, WIDE * B), lambda t: (0, t)),
+            pl.BlockSpec((1, rows), lambda t: (0, 0)),
+            pl.BlockSpec((2, rows, B), lambda t: (0, 0, 0)),
             pl.BlockSpec((rows, depth), lambda t: (0, 0)),
-            pl.BlockSpec((1, 1, 1, H, depth), even),
-            pl.BlockSpec((1, 1, 1, H, depth), odd),
-        ],
-        out_specs=pl.BlockSpec((rows, B), lambda t: (0, t)),
+        ] + blocks,
+        out_specs=pl.BlockSpec((rows, WIDE * B), lambda t: (0, t)),
         compiler_params=pltpu.CompilerParams(vmem_limit_bytes=48 * 2**20),
-    )(matrix, nugget, panel, rounded, side, side)
+    )(matrix, nugget, panel, rounded, *([side] * (2 * WIDE)))
 
 
 def body(kernel, nugget):
-    rows_here = kernel.shape[0]
-    tile, col = lax.axis_index("row"), lax.axis_index("col")
-    nugget = nugget.reshape(2, B)
-    strip = kernel[:, : 2 * B].reshape(rows_here, 2, B).transpose(1, 0, 2)
-    col_tile = jnp.arange(2)[:, None, None] * 4 + col
-    same = (
-        (col_tile == tile)
-        & (jnp.arange(rows_here)[None, :, None] == jnp.arange(B)[None, None, :])
-    )
-    strip = strip + jnp.where(same, nugget[0][None, None, :], 0.0)
-    panel, rounded, side = factor(strip)
+    nugget = nugget.reshape(1, kernel.shape[0])
+    panel, rounded, side = factor(kernel, nugget)
     return trailing(kernel, nugget, panel, rounded, side)
 
 

time: 179 us -> 167 us (0.933)
  Pallas kernels: 175 us -> 165 us
  local copies, waits for them, and re-layouts: 3.34 us -> 0.68 us
    pallas_call x1, Pallas kernels: 155 us -> 150 us  [factor(): pl.pallas_call(factor_kernel, out_shape=(jax.ShapeDtypeStruct((2, 2 * B,...]
    pallas_call x1, Pallas kernels: 19.4 us -> 14.8 us  [trailing(): pl.pallas_call(trailing_kernel, grid=(cols // (WIDE * B),), out_shape=jax...]
    slice x2 -> x0, local copies, waits for them, and re-layouts: 1.98 us -> none  [the longest x1 1.3 us: body(): strip = kernel[:, :2 * B].reshape(rows_here, 2, B).transpose(1, 0, 2)]
where the time goes in v4:
time: 167 us; the launch traced here: 166 us
  Pallas kernels  165 us (99%)
    pallas_call x1, Pallas kernels, factor(): pl.pallas_call(factor_kernel, out_shape=(jax.ShapeDtypeStruct((2, 2 * B,...  150 us
    pallas_call x1, Pallas kernels, trailing(): pl.pallas_call(trailing_kernel, grid=(cols // (WIDE * B),), out_shape=jax...  14.8 us

profile of v4, /device:TPU:1, one launch (start us, length us, event | category | flops | bytes accessed | tf_op | source)
XLA Modules:
  0.0 165.6 jit_solution(10601570678392896804)
XLA Ops:
  0.0 0.0 copy-start
  0.0 0.7 copy-done
  0.7 150.1 %shard_map.28 = (f32[2,512,256]{2,1,0:T(8,128)S(1)}, bf16[512,1792]{1,0:T(8,128)(2,1)S(1)}, bf16[2,4,4,128,1792]{4,3,2,1,0:T(8,128)(2,1)}) custom-call(f32[512,4096]{1,0:T(8,128)} %matrix_ref.3, f32[1,512]{1,0:T(1,128)S(1)} %bitcast.1), custom_call_target="tpu_custom_call" | custom-call | tf_op jit(solution)/shard_map/pallas_call | solution.py:569
  150.8 14.8 %shard_map.29 = f32[512,4096]{1,0:T(8,128)} custom-call(f32[512,4096]{1,0:T(8,128)} %matrix_ref.3, f32[1,512]{1,0:T(1,128)S(1)} %bitcast.2, f32[2,512,256]{2,1,0:T(8,128)S(1)} %get-tuple-element.8.panel_ref, bf16[512,1792]{1,0:T(8,128)(2,1)S(1)} %get-tuple-element.9.rounded_ref, ...), custom_call_target="tpu_custom_call" | custom-call | tf_op jit(solution)/shard_map/pallas_call | solution.py:647
Async XLA Ops:
  0.0 0.7 copy-start

commit v5 on v4

--- a/solution.py
+++ b/solution.py
@@ -8,7 +8,7 @@
 B = 256
 H = 128
 STEPS = 7
-WIDE = 4
+WIDE = 2
 F32 = jnp.float32
 BF16 = jnp.bfloat16
 MESH = pl.DeviceIdType.MESH
@@ -220,8 +220,8 @@
 
 
 def factor_kernel(
-    matrix_ref, nugget_ref, panel_ref, rounded_ref, side_ref,
-    tiles, strips, lead, inverse, diag, inv_half, mixed, acc,
+    matrix_ref, nugget_hbm, panel_ref, rounded_ref, side_ref,
+    nugget_ref, tiles, strips, lead, inverse, diag, inv_half, mixed, acc,
     fill_send, fill_recv, onward_send, onward_recv, keep_sem, share_send, share_recv, share_own,
     strip_send, strip_recv, lead_send, lead_recv, side_send, side_recv,
 ):
@@ -433,6 +433,8 @@
 
     for u in range(2):
         keep(u).start()
+    keep_nugget = pltpu.make_async_copy(nugget_hbm, nugget_ref, keep_sem.at[2])
+    keep_nugget.start()
 
     partners = [(row_of(core, major, (minor + d) % 4), col) for d in (1, 2, 3)]
     partners += [(row_of(core, (major + d) % 4, minor), col) for d in (1, 2, 3)]
@@ -446,6 +448,7 @@
         @pl.when((col <= to) & (row != to))
         def _(to=to):
             pl.semaphore_signal(barrier, inc=1, device_id=(to, col), device_id_type=MESH)
+    keep_nugget.wait()
     for u in range(2):
         keep(u).wait()
 
@@ -564,7 +567,7 @@
 
 def factor(matrix, nugget):
     vmem = pl.BlockSpec(memory_space=pltpu.VMEM)
-    anywhere = pl.BlockSpec(memory_space=pl.ANY)
+    anywhere = pl.BlockSpec(memory_space=pltpu.HBM)
     dma = pltpu.SemaphoreType.DMA
     return pl.pallas_call(
         factor_kernel,
@@ -573,9 +576,10 @@
             jax.ShapeDtypeStruct((2 * B, STEPS * B), BF16),
             jax.ShapeDtypeStruct((2, 4, 4, H, STEPS * B), BF16),
         ),
-        in_specs=[anywhere, vmem],
-        out_specs=(vmem, vmem, anywhere),
+        in_specs=[anywhere, anywhere],
+        out_specs=(vmem, vmem, vmem),
         scratch_shapes=[
+            pltpu.VMEM((1, 2 * B), F32),
             pltpu.VMEM((28, B, B), F32),
             pltpu.VMEM((4, 2, 2 * B, B), F32),
             pltpu.VMEM((28, B, B), BF16),
@@ -584,20 +588,18 @@
             pltpu.VMEM((H, H), F32),
             pltpu.VMEM((H, H), F32),
             pltpu.VMEM((2 * B, B), F32),
-            dma((2, 32)), dma((2,)), dma((2, 4)), dma((2, 4)), dma((2,)), dma((STEPS, 4)), dma((STEPS,)), dma,
+            dma((2, 32)), dma((2,)), dma((2, 4)), dma((2, 4)), dma((3,)), dma((STEPS, 4)), dma((STEPS,)), dma,
             dma((2, 6)), dma((2, 6)), dma((2, 13)), dma((2, 13)), dma((STEPS, 13)), dma((STEPS, 13)),
         ],
         compiler_params=pltpu.CompilerParams(
-            has_side_effects=True, collective_id=0, vmem_limit_bytes=48 * 2**20
+            has_side_effects=True, collective_id=0, vmem_limit_bytes=26 * 2**20
         ),
     )(matrix, nugget)
 
 
-def trailing_kernel(matrix_ref, nugget_ref, panel_ref, rounded_ref, *refs):
-    out_ref = refs[-1]
+def trailing_kernel(matrix_ref, nugget_ref, panel_ref, rounded_ref, side_ref, out_ref):
     tile, col = lax.axis_index("row"), lax.axis_index("col")
     for u in range(WIDE):
-        even_ref, odd_ref = refs[2 * u], refs[2 * u + 1]
         slot = pl.program_id(0) * WIDE + u
         col_tile = slot * 4 + col
         here = slice(u * B, (u + 1) * B)
@@ -607,8 +609,9 @@
             out_ref[:, here] = panel_ref[jnp.minimum(slot, 1)]
 
         @pl.when(col_tile >= STEPS)
-        def _(even_ref=even_ref, odd_ref=odd_ref, col_tile=col_tile, here=here):
-            side = jnp.concatenate([even_ref[0, 0, 0], odd_ref[0, 0, 0]], axis=0)
+        def _(slot=slot, col_tile=col_tile, here=here):
+            x, y = slot % 8 // 2, 2 * (slot % 2) + slot // 8
+            side = jnp.concatenate([side_ref[0, x, y], side_ref[1, y, x]], axis=0)
             out_ref[:, here] = matrix_ref[:, here] - dot_bf(rounded_ref[...], side, NT)
             for s in range(2):
                 @pl.when(col_tile == s * 32 + tile)
@@ -625,43 +628,23 @@
 
 def trailing(matrix, nugget, panel, rounded, side):
     rows, cols = matrix.shape
-    depth = rounded.shape[1]
-
-    def even(u):
-        def at(g):
-            t = g * WIDE + u
-            return (0, t % 8 // 2, 2 * (t % 2) + t // 8, 0, 0)
-
-        return at
-
-    def odd(u):
-        def at(g):
-            t = g * WIDE + u
-            return (1, 2 * (t % 2) + t // 8, t % 8 // 2, 0, 0)
-
-        return at
-
-    blocks = []
-    for u in range(WIDE):
-        blocks += [pl.BlockSpec((1, 1, 1, H, depth), even(u)), pl.BlockSpec((1, 1, 1, H, depth), odd(u))]
+    vmem = pl.BlockSpec(memory_space=pltpu.VMEM)
     return pl.pallas_call(
         trailing_kernel,
         grid=(cols // (WIDE * B),),
         out_shape=jax.ShapeDtypeStruct(matrix.shape, F32),
         in_specs=[
             pl.BlockSpec((rows, WIDE * B), lambda t: (0, t)),
-            pl.BlockSpec((1, rows), lambda t: (0, 0)),
-            pl.BlockSpec((2, rows, B), lambda t: (0, 0, 0)),
-            pl.BlockSpec((rows, depth), lambda t: (0, 0)),
-        ] + blocks,
+            vmem, vmem, vmem, vmem,
+        ],
         out_specs=pl.BlockSpec((rows, WIDE * B), lambda t: (0, t)),
-        compiler_params=pltpu.CompilerParams(vmem_limit_bytes=48 * 2**20),
-    )(matrix, nugget, panel, rounded, *([side] * (2 * WIDE)))
+        compiler_params=pltpu.CompilerParams(vmem_limit_bytes=20 * 2**20),
+    )(matrix, nugget, panel, rounded, side)
 
 
 def body(kernel, nugget):
     nugget = nugget.reshape(1, kernel.shape[0])
-    panel, rounded, side = factor(kernel, nugget)
+    panel, rounded, side = factor(pltpu.with_memory_space_constraint(kernel, pltpu.HBM), nugget)
     return trailing(kernel, nugget, panel, rounded, side)
 
 

time: 167 us -> 162 us (0.970)
  Pallas kernels: 165 us -> 159 us
    pallas_call x1, Pallas kernels: 150 us -> 147 us  [factor(): pl.pallas_call(factor_kernel, out_shape=(jax.ShapeDtypeStruct((2, 2 * B,...]
    pallas_call x1, Pallas kernels: 14.8 us -> 12 us  [trailing(): pl.pallas_call(trailing_kernel, grid=(cols // (WIDE * B),), out_shape=jax...]
where the time goes in v5:
time: 162 us; the launch traced here: 160 us
  Pallas kernels  159 us (98%)
    pallas_call x1, Pallas kernels, factor(): pl.pallas_call(factor_kernel, out_shape=(jax.ShapeDtypeStruct((2, 2 * B,...  147 us
    pallas_call x1, Pallas kernels, trailing(): pl.pallas_call(trailing_kernel, grid=(cols // (WIDE * B),), out_shape=jax...  12 us

profile of v5, /device:TPU:1, one launch (start us, length us, event | category | flops | bytes accessed | tf_op | source)
XLA Modules:
  0.0 159.7 jit_solution(1240072012874265172)
XLA Ops:
  0.0 0.0 copy-start
  0.0 0.0 copy-start.1
  0.0 0.8 copy-done.1
  0.8 146.9 %shard_map.28 = (f32[2,512,256]{2,1,0:T(8,128)S(1)}, bf16[512,1792]{1,0:T(8,128)(2,1)S(1)}, bf16[2,4,4,128,1792]{4,3,2,1,0:T(8,128)(2,1)S(1)}) custom-call(f32[512,4096]{1,0:T(8,128)} %matrix_ref.3, f32[1,512]{1,0:T(1,128)S(1)} %bitcast.1), custom_call_target="tpu_custom_call" | custom-call | tf_op jit(solution)/shard_map/pallas_call | solution.py:572
  147.7 0.0 copy-done
  147.7 12.0 %shard_map.29 = f32[512,4096]{1,0:T(8,128)} custom-call(f32[512,4096]{1,0:T(8,128)S(1)} %copy-done, f32[1,512]{1,0:T(1,128)S(1)} %bitcast.2, f32[2,512,256]{2,1,0:T(8,128)S(1)} %get-tuple-element.8.panel_ref, bf16[512,1792]{1,0:T(8,128)(2,1)S(1)} %get-tuple-element.9.rounded_ref, bf16[2,4,4,128,1792]{4,3,2,1,0:T(8,128)(2,1)S(1)} %get-tuple-element.10.side_ref), custom_call_target="tpu_custom_call" | custom-call | tf_op jit(solution)/shard_map/pallas_call | solution.py:632
Async XLA Ops:
  0.0 147.7 %copy-start = (f32[512,4096]{1,0:T(8,128)S(1)}, f32[512,4096]{1,0:T(8,128)}, u32[]{:S(2)}) copy-start(f32[512,4096]{1,0:T(8,128)} %matrix_ref.3) | copy-start | bytes 25165828
  0.0 0.8 copy-start.1

commit v6 on v5

--- a/solution.py
+++ b/solution.py
@@ -463,10 +463,10 @@
     for u in range(2):
         when(mine[u][2], lambda u=u: fill_own(u).start())
     onward_begin(0)
+    lead_begin(0)
+    lead_walk.second(0)
+    onward_begin(1)
     strip_begin(0)
-    lead_begin(0)
-    onward_begin(1)
-    lead_walk.second(0)
     lead_walk.third(0)
     lead_walk.fourth(0)
     lead_walk.finish(0)

time: 162 us -> 161 us (level)
  no operation moved by 1% of the time
where the time goes in v6:
time: 161 us; the launch traced here: 159 us
  Pallas kernels  158 us (98%)
    pallas_call x1, Pallas kernels, factor(): pl.pallas_call(factor_kernel, out_shape=(jax.ShapeDtypeStruct((2, 2 * B,...  146 us
    pallas_call x1, Pallas kernels, trailing(): pl.pallas_call(trailing_kernel, grid=(cols // (WIDE * B),), out_shape=jax...  12 us

profile of v6, /device:TPU:1, one launch (start us, length us, event | category | flops | bytes accessed | tf_op | source)
XLA Modules:
  0.0 159.2 jit_solution(15183757207250485255)
XLA Ops:
  0.0 0.0 copy-start
  0.0 0.0 copy-start.1
  0.0 0.8 copy-done.1
  0.8 146.4 %shard_map.28 = (f32[2,512,256]{2,1,0:T(8,128)S(1)}, bf16[512,1792]{1,0:T(8,128)(2,1)S(1)}, bf16[2,4,4,128,1792]{4,3,2,1,0:T(8,128)(2,1)S(1)}) custom-call(f32[512,4096]{1,0:T(8,128)} %matrix_ref.3, f32[1,512]{1,0:T(1,128)S(1)} %bitcast.1), custom_call_target="tpu_custom_call" | custom-call | tf_op jit(solution)/shard_map/pallas_call | solution.py:572
  147.3 0.0 copy-done
  147.3 12.0 %shard_map.29 = f32[512,4096]{1,0:T(8,128)} custom-call(f32[512,4096]{1,0:T(8,128)S(1)} %copy-done, f32[1,512]{1,0:T(1,128)S(1)} %bitcast.2, f32[2,512,256]{2,1,0:T(8,128)S(1)} %get-tuple-element.8.panel_ref, bf16[512,1792]{1,0:T(8,128)(2,1)S(1)} %get-tuple-element.9.rounded_ref, bf16[2,4,4,128,1792]{4,3,2,1,0:T(8,128)(2,1)S(1)} %get-tuple-element.10.side_ref), custom_call_target="tpu_custom_call" | custom-call | tf_op jit(solution)/shard_map/pallas_call | solution.py:632
Async XLA Ops:
  0.0 147.3 %copy-start = (f32[512,4096]{1,0:T(8,128)S(1)}, f32[512,4096]{1,0:T(8,128)}, u32[]{:S(2)}) copy-start(f32[512,4096]{1,0:T(8,128)} %matrix_ref.3) | copy-start | bytes 25165828
  0.0 0.8 copy-start.1
